TPU v7x, 32 devices: a whole 2x2x4 slice. The times are simulated.
32 devices in a mesh: groups: 2 (over y), ctx: 4 (over z), tp: 4 (over x, core).
Axes of the slice: x: 2, y: 2, z: 4, core: 2. Of those that a mesh axis runs over, the one named last changes fastest.
Arguments:
- x_input: bfloat16 [4096, 4096], P(('groups', 'ctx', 'tp')), parts along dimension 0, may hold values from -6 to 6
- bc_input: bfloat16 [4096, 2, 1024], P(('groups', 'ctx', 'tp')), parts along dimension 0, may hold values from -6 to 6
- z_input: bfloat16 [4096, 4096], P(('groups', 'ctx', 'tp')), parts along dimension 0, may hold values from -100 to 100, as said below
- dt_input: bfloat16 [4096, 64], P(('groups', 'ctx', 'tp')), parts along dimension 0, may hold values from -1.5 to 0.5
- x_kernel: float32 [4, 4096], replicated, may hold values from -2.5 to 2.5
- x_bias: float32 [4096], replicated, may hold values from -3 to 3
- bc_kernel: float32 [4, 2, 1024], replicated, may hold values from -2.5 to 2.5
- bc_bias: float32 [2, 1024], replicated, may hold values from -3 to 3
- dt_bias: float32 [64], P('tp'), may hold values from -1 to 1
- a_log: float32 [64], P('tp'), as said below
- d_skip: float32 [64], P('tp'), may hold values from 0.5 to 2
- norm_gain: float32 [4096], P('tp'), may hold values from 0.5 to 1.5
Outputs:
- gated_out: bfloat16 [4096, 4096], P(('groups', 'ctx'), 'tp'), parts along dimension 0
There are 2 independent parts, one for each index of `groups`. A program takes and returns all parts, laid end to end along the dimension named above; an argument that names none is the same for every part. Nothing has to cross between parts.
Inputs may be any that keep to these rules, and one draw needn't show every extreme that they name: Every entry of z_input is a product of a random sign and magnitude with a token factor and a head factor. Each head's rate exp(a_log) lies between 0.2 / 2048 and 0.1.
All inputs are finite; a program needn't handle non-finite values.
Results may differ from a plain program's by a relative error of at most 0.0034.
Values may be sent and summed in bfloat16 or wider, within the bound.
No kernel may reach another device: no remote copies, remote signals or barrier semaphores. Data moves between devices by JAX's collectives and lax.ppermute only.
A program may use at most 64 MiB of HBM per device.

v0:
```python
import jax
import jax.numpy as jnp
from jax import lax
from jax.sharding import PartitionSpec as P

HEADS = 64
HEAD_DIM = 64
STATE_DIM = 128
GROUPS = 8
CONV_TAPS = 4
BLOCK_LEN = 256


def from_behind(value, axis, steps):
    count = lax.axis_size(axis)
    leading, last = (max(0, -steps), min(count, count - steps))
    return lax.ppermute(value, axis, [(source, source + steps) for source in range(leading, last)])


def carried_in(value, axis, join, neutral):
    count, mine = (lax.axis_size(axis), lax.axis_index(axis))
    pieces = jax.tree.map(lambda part: lax.all_gather(part, axis), value)
    running = jax.tree.map(
        lambda part, zero: jnp.full_like(part, 0) + jnp.asarray(zero, part.dtype), value, neutral
    )

    def turn(position, running):
        longer = join(running, jax.tree.map(lambda part: part[position], pieces))
        return jax.tree.map(lambda new, old: jnp.where(position < mine, new, old), longer, running)

    return lax.fori_loop(0, count - 1, turn, running)


def conv_valid(padded, kernel_taps, kernel_bias):
    out_count = padded.shape[0] - (CONV_TAPS - 1)
    summed = kernel_bias + jnp.zeros(padded[:out_count].shape, jnp.float32)
    for offset in range(CONV_TAPS):
        summed = summed + kernel_taps[offset] * padded[offset : offset + out_count].astype(
            jnp.float32
        )
    return jax.nn.silu(summed).astype(jnp.bfloat16)


def join_state(earlier, later):
    return (earlier[0] * later[0], later[0][:, None, None] * earlier[1] + later[1])


def shards(
    x_input,
    bc_input,
    z_input,
    dt_input,
    x_kernel,
    x_bias,
    bc_kernel,
    bc_bias,
    dt_bias,
    a_log,
    d_skip,
    norm_gain,
):
    tp_size = lax.axis_size("tp")
    tp_place = lax.axis_index("tp")
    row_count = x_input.shape[0]
    ctx_rows = row_count * tp_size
    heads_dev = HEADS // tp_size
    per_group = HEADS // GROUPS
    groups_dev = heads_dev // per_group
    width_dev = heads_dev * HEAD_DIM
    rim_rows = CONV_TAPS - 1
    first_group = tp_place * groups_dev
    x_send = x_input.reshape(row_count, 1, tp_size, width_dev)
    bc_send = bc_input.reshape(row_count, 2, tp_size, groups_dev * STATE_DIM)
    step_send = dt_input.reshape(row_count, 1, tp_size, heads_dev)
    gate_send = z_input.reshape(row_count, 1, tp_size, width_dev)
    x_back, bc_back, step_back, gate_back = (
        lax.all_to_all(x_send, "tp", split_axis=2, concat_axis=0, tiled=True),
        lax.all_to_all(bc_send, "tp", split_axis=2, concat_axis=0, tiled=True),
        lax.all_to_all(step_send, "tp", split_axis=2, concat_axis=0, tiled=True),
        lax.all_to_all(gate_send, "tp", split_axis=2, concat_axis=0, tiled=True),
    )
    x_owned = x_back.reshape(ctx_rows, width_dev)
    bc_owned = bc_back.reshape(ctx_rows, 2, groups_dev * STATE_DIM)
    owned_rim = from_behind(
        (x_owned[ctx_rows - rim_rows :], bc_owned[ctx_rows - rim_rows :]), "ctx", 1
    )
    x_taps = lax.dynamic_slice_in_dim(x_kernel, tp_place * width_dev, width_dev, 1)
    x_shift = lax.dynamic_slice_in_dim(x_bias, tp_place * width_dev, width_dev, 0)
    bc_taps = lax.dynamic_slice_in_dim(
        bc_kernel, first_group * STATE_DIM, groups_dev * STATE_DIM, 2
    )
    bc_shift = lax.dynamic_slice_in_dim(bc_bias, first_group * STATE_DIM, groups_dev * STATE_DIM, 1)
    x_conv = conv_valid(jnp.concatenate([owned_rim[0], x_owned], axis=0), x_taps, x_shift)
    bc_conv = conv_valid(jnp.concatenate([owned_rim[1], bc_owned], axis=0), bc_taps, bc_shift)
    step_size = jax.nn.softplus(
        step_back.reshape(ctx_rows, heads_dev).astype(jnp.float32) + dt_bias
    )
    log_decay = step_size * -jnp.exp(a_log)
    block_count = ctx_rows // BLOCK_LEN
    x_blocks = x_conv.reshape(block_count, BLOCK_LEN, heads_dev, HEAD_DIM)
    bc_blocks = bc_conv.reshape(block_count, BLOCK_LEN, 2, groups_dev, STATE_DIM)
    step_blocks = step_size.reshape(block_count, BLOCK_LEN, heads_dev)
    log_blocks = log_decay.reshape(block_count, BLOCK_LEN, heads_dev)
    positions = jnp.arange(BLOCK_LEN)
    causal = positions[:, None] >= positions[None, :]

    def block_terms(items):
        x_block, bc_block, step_block, log_block = items
        decay_sums = jnp.cumsum(log_block, axis=0)
        b_block = bc_block[:, 0]
        c_block = bc_block[:, 1]
        score_groups = jnp.einsum(
            "tgn,sgn->gts", c_block, b_block, preferred_element_type=jnp.float32
        )
        score_heads = jnp.repeat(score_groups, per_group, axis=0)
        decay_cols = decay_sums.T
        gaps = decay_cols[:, :, None] - decay_cols[:, None, :]
        decays = jnp.where(causal[None], jnp.exp(jnp.where(causal[None], gaps, 0.0)), 0.0)
        weights = (score_heads * decays * step_block.T[:, None, :]).astype(jnp.bfloat16)
        intra_out = jnp.einsum("hts,shp->thp", weights, x_block, preferred_element_type=jnp.float32)
        tail_scale = jnp.exp(decay_sums[-1][None, :] - decay_sums) * step_block
        scaled_x = (tail_scale[:, :, None] * x_block.astype(jnp.float32)).astype(jnp.bfloat16)
        b_heads = jnp.repeat(b_block, per_group, axis=1)
        contrib_state = jnp.einsum(
            "shp,shn->hpn", scaled_x, b_heads, preferred_element_type=jnp.float32
        )
        return (intra_out, contrib_state, decay_sums)

    intra_all, contrib_all, decay_all = lax.map(
        block_terms, (x_blocks, bc_blocks, step_blocks, log_blocks)
    )
    block_logs = decay_all[:, -1]

    def local_chain(carried, items):
        contrib_state, block_log = items
        return (jnp.exp(block_log)[:, None, None] * carried + contrib_state, carried)

    zero_state = jnp.zeros((heads_dev, HEAD_DIM, STATE_DIM), jnp.float32)
    local_totals, local_starts = lax.scan(local_chain, zero_state, (contrib_all, block_logs))
    device_decay = jnp.exp(jnp.sum(block_logs, axis=0))
    prior_logs = jnp.cumsum(block_logs, axis=0) - block_logs
    earlier_decay, start_state = carried_in(
        (device_decay, local_totals),
        "ctx",
        join_state,
        (jnp.ones_like(device_decay), jnp.zeros_like(local_totals)),
    )
    block_states = jnp.exp(prior_logs)[:, :, None, None] * start_state[None] + local_starts
    c_groups = bc_blocks[:, :, 1].astype(jnp.float32)
    states_grouped = block_states.reshape(block_count, groups_dev, per_group, HEAD_DIM, STATE_DIM)
    inter_raw = jnp.einsum(
        "btgn,bgkpn->btgkp", c_groups, states_grouped, precision=lax.Precision.HIGHEST
    )
    inter_out = jnp.exp(decay_all)[..., None] * inter_raw.reshape(
        block_count, BLOCK_LEN, heads_dev, HEAD_DIM
    )
    ssm_out = intra_all + inter_out + d_skip[:, None] * x_blocks.astype(jnp.float32)
    ssm_out = ssm_out.reshape(ctx_rows, width_dev)
    gate_owned = gate_back.reshape(ctx_rows, width_dev)
    gated = ssm_out * jax.nn.silu(gate_owned.astype(jnp.float32))
    grouped = gated.reshape(ctx_rows, groups_dev, -1)
    mean_square = jnp.mean(grouped * grouped, axis=-1, keepdims=True)
    normed = (grouped * lax.rsqrt(mean_square + 1e-05)).reshape(ctx_rows, width_dev) * norm_gain
    return normed.astype(jnp.bfloat16)


def solution(mesh):
    in_specs = (
        P(("groups", "ctx", "tp"), None),
        P(("groups", "ctx", "tp"), None, None),
        P(("groups", "ctx", "tp"), None),
        P(("groups", "ctx", "tp"), None),
        P(),
        P(),
        P(),
        P(),
        P("tp"),
        P("tp"),
        P("tp"),
        P("tp"),
    )
    out_specs = P(("groups", "ctx"), "tp")
    return jax.shard_map(shards, mesh=mesh, in_specs=in_specs, out_specs=out_specs, check_vma=False)
```

profile of v0, /device:TPU:0, one launch (start us, length us, event | category | flops | bytes accessed | tf_op | source)
XLA Modules:
  0.0 141.4 jit_solution(14970521830975234270)
XLA Ops:
  6.5 4.4 %all-to-all-start.2 = ((bf16[128,1,4,16]{0,3,1,2:T(8,128)(2,1)}), bf16[128,1,4,16]{0,3,1,2:T(8,128)(2,1)S(1)}, u32[]{:S(2)}, u32[]{:S(2)}) async-start(bf16[128,1,4,16]{0,3,1,2:T(8,128)(2,1)} %bitcast.258), calls=%async_computation.2 | async-start | bytes 32768 | tf_op jit(solution)/shard_map/all_to_all | solution.py:79
  10.9 1.4 copy.101
  13.1 1.7 %all-to-all-done.2 = bf16[128,1,4,16]{0,3,1,2:T(8,128)(2,1)S(1)} async-done(((bf16[128,1,4,16]{0,3,1,2:T(8,128)(2,1)}), bf16[128,1,4,16]{0,3,1,2:T(8,128)(2,1)S(1)}, u32[]{:S(2)}, u32[]{:S(2)}) %all-to-all-start.2) | async-done | bytes 16416 | tf_op jit(solution)/shard_map/all_to_all | solution.py:79
  14.8 3.5 %all-to-all-start.1 = ((bf16[128,2,4,256]{0,3,1,2:T(8,128)(2,1)}), bf16[128,2,4,256]{0,3,1,2:T(8,128)(2,1)S(1)}, u32[]{:S(2)}, u32[]{:S(2)}) async-start(bf16[128,2,4,256]{0,3,1,2:T(8,128)(2,1)} %copy.102), calls=%async_computation.1 | async-start | bytes 1048576 | tf_op jit(solution)/shard_map/all_to_all | solution.py:78
  18.3 1.3 copy.99
  21.3 5.7 %all-to-all-done.1 = bf16[128,2,4,256]{0,3,1,2:T(8,128)(2,1)S(1)} async-done(((bf16[128,2,4,256]{0,3,1,2:T(8,128)(2,1)}), bf16[128,2,4,256]{0,3,1,2:T(8,128)(2,1)S(1)}, u32[]{:S(2)}, u32[]{:S(2)}) %all-to-all-start.1) | async-done | bytes 524320 | tf_op jit(solution)/shard_map/all_to_all | solution.py:78
  27.0 3.5 %all-to-all-start = ((bf16[128,1,4,1024]{0,3,1,2:T(8,128)(2,1)}), bf16[128,1,4,1024]{0,3,1,2:T(8,128)(2,1)S(1)}, u32[]{:S(2)}, u32[]{:S(2)}) async-start(bf16[128,1,4,1024]{0,3,1,2:T(8,128)(2,1)} %bitcast.1), calls=%async_computation | async-start | bytes 2097152 | tf_op jit(solution)/shard_map/all_to_all | solution.py:77
  31.0 3.9 %collective-permute-start.1 = (bf16[3,2,256]{2,0,1:T(4,128)(2,1)S(1)}, bf16[3,2,256]{2,0,1:T(4,128)(2,1)S(1)}, u32[]{:S(2)}, u32[]{:S(2)}) collective-permute-start(bf16[3,2,256]{2,0,1:T(4,128)(2,1)S(1)} %slice.106), channel_id=1, source_target_pairs={{0,4},{4,8},{8,12},{1,5},{5,9},{9,13},{2,6},{6,10},{10,14},{3,7},{... | collective-permute-start | bytes 9224 | tf_op jit(solution)/shard_map/ppermute | solution.py:17
  35.1 9.9 %all-to-all-done = bf16[128,1,4,1024]{0,3,1,2:T(8,128)(2,1)S(1)} async-done(((bf16[128,1,4,1024]{0,3,1,2:T(8,128)(2,1)}), bf16[128,1,4,1024]{0,3,1,2:T(8,128)(2,1)S(1)}, u32[]{:S(2)}, u32[]{:S(2)}) %all-to-all-start) | async-done | bytes 1048608 | tf_op jit(solution)/shard_map/all_to_all | solution.py:77
  46.8 3.9 %collective-permute-start = (bf16[3,1024]{0,1:T(8,128)(2,1)}, bf16[3,1024]{0,1:T(8,128)(2,1)S(1)}, u32[]{:S(2)}, u32[]{:S(2)}) collective-permute-start(bf16[3,1024]{0,1:T(8,128)(2,1)} %slice.101), channel_id=1, source_target_pairs={{0,4},{4,8},{8,12},{1,5},{5,9},{9,13},{2,6},{6,10},{10,14},{3,7},{... | collective-permute-start | bytes 18440 | tf_op jit(solution)/shard_map/ppermute | solution.py:17
  51.6 4.7 %collective-permute-done = bf16[3,1024]{0,1:T(8,128)(2,1)S(1)} collective-permute-done((bf16[3,1024]{0,1:T(8,128)(2,1)}, bf16[3,1024]{0,1:T(8,128)(2,1)S(1)}, u32[]{:S(2)}, u32[]{:S(2)}) %collective-permute-start) | collective-permute-done | bytes 6176 | tf_op jit(solution)/shard_map/ppermute | solution.py:17
  56.3 2.7 %multiply_convert_fusion.2 = bf16[512,1024]{0,1:T(8,128)(2,1)S(1)} fusion(bf16[512,1024]{0,1:T(8,128)(2,1)S(1)} %bitcast.244, bf16[3,1024]{0,1:T(8,128)(2,1)S(1)} %collective-permute-done, f32[1024]{0:T(1024)S(1)} %bitcast.257, f32[1024]{0:T(1024)S(1)} %bitcast.255, f32[1024]{0:T(1024)S(1)} %bitcast.256, f32[1024]{0:T(1024)S(1)} %bitcast.254, ...), kind=kLoop, calls=%fused_computation.53 | loop fusion | flops 13631488 | bytes 2123776 | tf_op jit(solution)/shard_map/convert_element_type | solution.py:41
  60.4 9.9 %while.43 = (s32[]{:T(128)}, f32[2,256,16,64]{1,3,2,0:T(8,128)}, f32[2,16,64,128]{3,2,1,0:T(8,128)S(1)}, f32[2,256,16]{1,2,0:T(8,128)S(1)}, bf16[2,256,16,64]{1,...) while((s32[]{:T(128)}, f32[2,256,16,64]{1,3,2,0:T(8,128)}, ...), condition=%wide.region_3.4_spmd.clone.clone, body=%wide.region_0.3_spmd.clone.clone.sunk | while | flops 242565168 | bytes 28922288 | solution.py:129
  61.9 1.3 fusion.48
  66.8 1.3 fusion.48
  71.9 2.3 %copy.113 = bf16[128,4096]{0,1:T(8,128)(2,1)} copy(bf16[128,4096]{1,0:T(8,128)(2,1)} %param.20) | data formatting | bytes 2097152 | tf_op args[2]
  74.2 3.5 %all-to-all-start.3 = ((bf16[128,1,4,1024]{0,3,1,2:T(8,128)(2,1)}), bf16[128,1,4,1024]{0,3,1,2:T(8,128)(2,1)S(1)}, u32[]{:S(2)}, u32[]{:S(2)}) async-start(bf16[128,1,4,1024]{0,3,1,2:T(8,128)(2,1)} %bitcast.247), calls=%async_computation.3 | async-start | bytes 2097152 | tf_op jit(solution)/shard_map/all_to_all | solution.py:80
  79.0 13.1 %all-to-all-done.3 = bf16[128,1,4,1024]{0,3,1,2:T(8,128)(2,1)S(1)} async-done(((bf16[128,1,4,1024]{0,3,1,2:T(8,128)(2,1)}), bf16[128,1,4,1024]{0,3,1,2:T(8,128)(2,1)S(1)}, u32[]{:S(2)}, u32[]{:S(2)}) %all-to-all-start.3) | async-done | bytes 1048608 | tf_op jit(solution)/shard_map/all_to_all | solution.py:80
  92.2 1.4 copy.114
  93.6 2.8 %reshape.179 = f32[2,256,16,64]{1,0,3,2:T(2,128)} reshape(f32[4,128,1,1,1024]{1,0,4,3,2:T(4,128)S(1)} %copy.114) | data formatting | bytes 4194304 | tf_op jit(solution)/shard_map/convert_element_type | solution.py:160
  96.6 13.6 %all-reduce = f32[64]{0:T(128)S(1)} all-reduce(f32[64]{0:T(128)S(1)} %exponential_dynamic-update-slice_fusion), channel_id=2, replica_groups=mesh['groups'=2,'ctx'=4,'tp'=4] {'ctx'}, use_global_device_ids=true, to_apply=%add | all-reduce | flops 64 | bytes 512
  110.3 9.0 %all-gather.4.cloned.1.call-done = f32[64,64,128]{2,1,0:T(8,128)} async-done(((f32[16,64,128]{2,1,0:T(8,128)}), f32[64,64,128]{2,1,0:T(8,128)}) %all-gather.4.cloned.1.call-update) | async-done | bytes 2097168 | tf_op jit(solution)/shard_map/all_gather | solution.py:22
  119.3 3.6 %while.45 = (s32[]{:T(128)}, f32[16,64,128]{2,1,0:T(8,128)S(1)}, s32[]{:T(128)}, f32[4,16]{1,0:T(4,128)S(1)}, f32[4,16,64,128]{3,2,1,0:T(8,128)}, /*index=5*/s32[]{:T(128)}, s32[]{:T(128)}) while((s32[]{:T(128)}, f32[16,64,128]{2,1,0:T(8,128)S(1)}, s32[]{:T(128)}, f32[4,16]{1,0:T(4,128)S(1)}, f32[4,16,64,128]{3,2,1,0:T(8,128)}, ...), condition=%wide.region_9.10_spmd.clone, body=%wide.region_8.9_spmd.clone.sunk | while | flops 524292 | bytes 1573161 | solution.py:31
  119.3 1.2 fusion.52
  120.5 1.2 fusion.52
  121.7 1.2 fusion.52
  122.9 1.5 %multiply_add_fusion.1 = f32[2,16,64,128]{3,2,1,0:T(8,128)S(1)} fusion(f32[2,16,64,128]{3,2,1,0:T(8,128)} %copy-done.5, f32[16,64,128]{2,1,0:T(8,128)S(1)} %get-tuple-element.183, f32[2,16]{1,0:T(2,128)S(1)} %subtract_exponential_fusion), kind=kLoop, calls=%fused_computation.63 | loop fusion | flops 524288 | bytes 2621568 | tf_op jit(solution)/shard_map/add | solution.py:148
  126.5 1.2 multiply_reduce_fusion
  127.6 1.6 %copy.112 = f32[2,256,16,64]{1,0,3,2:T(2,128)S(1)} copy(f32[2,256,16,64]{1,3,2,0:T(8,128)S(1)} %get-tuple-element.348) | data formatting | bytes 4194304 | tf_op jit(solution)/shard_map/add | solution.py:157
  129.3 1.5 %copy.132 = f32[128,8,2,256]{3,1,2,0:T(8,128)} copy(f32[128,8,2,256]{3,2,1,0:T(2,128)S(1)} %bitcast.242) | data formatting | bytes 4194304
  130.9 2.3 %fusion.24 = bf16[512,1024]{0,1:T(8,128)(2,1)S(1)} fusion(f32[512,1024]{0,1:T(8,128)} %bitcast.240, f32[128,8,4,128]{3,2,1,0:T(4,128)S(1)} %bitcast.239, f32[1024]{0:T(1024)S(1)} %copy-done.11, f32[512,2]{0,1:T(2,128)S(1)} %add_rsqrt_fusion), kind=kLoop, calls=%fused_computation.54 | loop fusion | flops 4194304 | bytes 5251072 | tf_op jit(solution)/shard_map/convert_element_type | solution.py:164
  133.2 1.3 copy.119
  (128 shorter events, 19.2 us)
Async XLA Ops:
  6.5 24.1 %copy-start = (f32[2,1024]{1,0:T(2,128)S(1)}, f32[2,1024]{1,0:T(2,128)}, u32[]{:S(2)}) copy-start(f32[2,1024]{1,0:T(2,128)} %param.25) | copy-start | bytes 24580
  6.5 11.7 %copy-start.9 = (bf16[128,4096]{1,0:T(8,128)(2,1)S(1)}, bf16[128,4096]{1,0:T(8,128)(2,1)}, u32[]{:S(2)}) copy-start(bf16[128,4096]{1,0:T(8,128)(2,1)} %param.18) | copy-start | bytes 3145732
  6.5 8.2 %all-to-all-start.2 = ((bf16[128,1,4,16]{0,3,1,2:T(8,128)(2,1)}), bf16[128,1,4,16]{0,3,1,2:T(8,128)(2,1)S(1)}, u32[]{:S(2)}, u32[]{:S(2)}) async-start(bf16[128,1,4,16]{0,3,1,2:T(8,128)(2,1)} %bitcast.258), calls=%async_computation.2 | async-start | bytes 32768 | tf_op jit(solution)/shard_map/all_to_all | solution.py:79
  14.8 12.3 %all-to-all-start.1 = ((bf16[128,2,4,256]{0,3,1,2:T(8,128)(2,1)}), bf16[128,2,4,256]{0,3,1,2:T(8,128)(2,1)S(1)}, u32[]{:S(2)}, u32[]{:S(2)}) async-start(bf16[128,2,4,256]{0,3,1,2:T(8,128)(2,1)} %copy.102), calls=%async_computation.1 | async-start | bytes 1048576 | tf_op jit(solution)/shard_map/all_to_all | solution.py:78
  18.3 12.3 %copy-start.14 = (f32[16]{0:T(128)S(1)}, f32[16]{0:T(128)}, u32[]{:S(2)}) copy-start(f32[16]{0:T(128)} %param.27) | copy-start | bytes 196
  19.6 15.3 %copy-start.12 = (f32[16]{0:T(128)S(1)}, f32[16]{0:T(128)}, u32[]{:S(2)}) copy-start(f32[16]{0:T(128)} %param.26) | copy-start | bytes 196
  27.0 17.9 %all-to-all-start = ((bf16[128,1,4,1024]{0,3,1,2:T(8,128)(2,1)}), bf16[128,1,4,1024]{0,3,1,2:T(8,128)(2,1)S(1)}, u32[]{:S(2)}, u32[]{:S(2)}) async-start(bf16[128,1,4,1024]{0,3,1,2:T(8,128)(2,1)} %bitcast.1), calls=%async_computation | async-start | bytes 2097152 | tf_op jit(solution)/shard_map/all_to_all | solution.py:77
  30.6 88.8 %all-gather.4.cloned.1.call-start = ((), (), s32[]{:S(2)}) async-start(), calls=%async_computation.4 | async-start | bytes 2621440 | tf_op jit(solution)/shard_map/all_gather | solution.py:22
  31.0 19.8 %collective-permute-start.1 = (bf16[3,2,256]{2,0,1:T(4,128)(2,1)S(1)}, bf16[3,2,256]{2,0,1:T(4,128)(2,1)S(1)}, u32[]{:S(2)}, u32[]{:S(2)}) collective-permute-start(bf16[3,2,256]{2,0,1:T(4,128)(2,1)S(1)} %slice.106), channel_id=1, source_target_pairs={{0,4},{4,8},{8,12},{1,5},{5,9},{9,13},{2,6},{6,10},{10,14},{3,7},{... | collective-permute-start | bytes 9224 | tf_op jit(solution)/shard_map/ppermute | solution.py:17
  45.8 10.6 %dynamic-slice-start = ((f32[4096]{0:T(1024)}, s32[]{:T(128)}), f32[1024]{0:T(1024)S(1)}, s32[]{:S(2)}) async-start(f32[4096]{0:T(1024)} %param.23, s32[]{:T(128)} %select_n.43), calls=%async_computation.5 | async-start | bytes 8704 | tf_op jit(solution)/shard_map/dynamic_slice | solution.py:88
  46.8 9.5 %collective-permute-start = (bf16[3,1024]{0,1:T(8,128)(2,1)}, bf16[3,1024]{0,1:T(8,128)(2,1)S(1)}, u32[]{:S(2)}, u32[]{:S(2)}) collective-permute-start(bf16[3,1024]{0,1:T(8,128)(2,1)} %slice.101), channel_id=1, source_target_pairs={{0,4},{4,8},{8,12},{1,5},{5,9},{9,13},{2,6},{6,10},{10,14},{3,7},{... | collective-permute-start | bytes 18440 | tf_op jit(solution)/shard_map/ppermute | solution.py:17
  59.3 1.0 copy-start.2
  59.3 1.1 copy-start.10
  61.5 1.6 %copy-start.6 = (f32[2,256,16,64]{1,3,2,0:T(8,128)S(1)}, f32[2,256,16,64]{1,3,2,0:T(8,128)}, u32[]{:S(2)}) copy-start(f32[2,256,16,64]{1,3,2,0:T(8,128)} %get-tuple-element.493) | copy-start | bytes 6291460 | tf_op jit(solution)/shard_map/while
  63.9 1.3 copy-start.7
  66.5 1.6 %copy-start.6 = (f32[2,256,16,64]{1,3,2,0:T(8,128)S(1)}, f32[2,256,16,64]{1,3,2,0:T(8,128)}, u32[]{:S(2)}) copy-start(f32[2,256,16,64]{1,3,2,0:T(8,128)} %get-tuple-element.493) | copy-start | bytes 6291460 | tf_op jit(solution)/shard_map/while
  68.9 1.3 copy-start.7
  71.0 0.8 copy-start.1
  71.1 3.1 %copy-start.5 = (f32[2,16,64,128]{3,2,1,0:T(8,128)}, f32[2,16,64,128]{3,2,1,0:T(8,128)S(1)}, u32[]{:S(2)}) copy-start(f32[2,16,64,128]{3,2,1,0:T(8,128)S(1)} %get-tuple-element.184) | copy-start | bytes 3145732
  71.9 5.8 %copy-start.15 = (u32[32]{0:T(128)S(1)}, u32[32]{0:T(128)}, u32[]{:S(2)}) copy-start(u32[32]{0:T(128)} %constant.96) | copy-start | bytes 388
  74.2 17.9 %all-to-all-start.3 = ((bf16[128,1,4,1024]{0,3,1,2:T(8,128)(2,1)}), bf16[128,1,4,1024]{0,3,1,2:T(8,128)(2,1)S(1)}, u32[]{:S(2)}, u32[]{:S(2)}) async-start(bf16[128,1,4,1024]{0,3,1,2:T(8,128)(2,1)} %bitcast.247), calls=%async_computation.3 | async-start | bytes 2097152 | tf_op jit(solution)/shard_map/all_to_all | solution.py:80
  122.9 2.6 %copy-start.8 = (f32[2,256,16,64]{1,3,2,0:T(8,128)S(1)}, f32[2,256,16,64]{1,3,2,0:T(8,128)}, u32[]{:S(2)}) copy-start(f32[2,256,16,64]{1,3,2,0:T(8,128)} %get-tuple-element.179) | copy-start | bytes 6291460
  124.5 1.3 copy-start.3
  124.5 2.0 %copy-start.4 = (f32[2,256,16,64]{1,0,3,2:T(2,128)S(1)}, f32[2,256,16,64]{1,0,3,2:T(2,128)}, u32[]{:S(2)}) copy-start(f32[2,256,16,64]{1,0,3,2:T(2,128)} %reshape.179) | copy-start | bytes 6291460
  124.5 2.0 %copy-start.13 = (f32[16]{0:T(128)S(1)}, f32[16]{0:T(128)}, u32[]{:S(2)}) copy-start(f32[16]{0:T(128)} %param.28) | copy-start | bytes 196
  129.3 1.6 %copy-start.11 = (f32[1024]{0:T(1024)S(1)}, f32[1024]{0:T(1024)}, u32[]{:S(2)}) copy-start(f32[1024]{0:T(1024)} %param.29) | copy-start | bytes 12292
Sparse Core Ops, SparseCore 0:
  72.0 47.2 all-gather.3
where the time goes:
time: 142 us; the launch traced here: 141 us
  waiting for transfers between devices  44 us (31%)
  local copies, waits for them, and re-layouts  25.3 us (18%)
  starting transfers between devices  22.8 us (16%)
  other arithmetic  17.2 us (12%)
  between operations  14.4 us (10%)
  blocking collectives  13.6 us (10%)
  matrix products  3.56 us (3%)
    unnamed x1, blocking collectives  13.6 us
    all_to_all x1, waiting for transfers between devices, shards(): lax.all_to_all(gate_send, 'tp', split_axis=2, concat_axis=0, tiled=True)  13.1 us
    unnamed x37, local copies, waits for them, and re-layouts  10 us
    all_to_all x1, waiting for transfers between devices, shards(): lax.all_to_all(x_send, 'tp', split_axis=2, concat_axis=0, tiled=True)  9.86 us
    all_gather x1, waiting for transfers between devices, carried_in(): pieces = jax.tree.map(lambda part: lax.all_gather(part, axis), value)  9.01 us
    ppermute x2, starting transfers between devices, from_behind(): lax.ppermute(value, axis, [(source, source + steps) for source in range(l...  7.89 us
    all_to_all x1, waiting for transfers between devices, shards(): lax.all_to_all(bc_send, 'tp', split_axis=2, concat_axis=0, tiled=True)  5.71 us
    ppermute x2, waiting for transfers between devices, from_behind(): lax.ppermute(value, axis, [(source, source + steps) for source in range(l...  4.69 us
  transfers between devices with their start and end apart: 7, of which 6 were waited for; matrix products, arithmetic and copies ran while one was open for 11% of the time, Pallas kernels for 0%

commit v1 on v0

v1 whole, which is shorter than its diff:
```python
import functools

import jax
import jax.numpy as jnp
from jax import lax
from jax.experimental import pallas as pl
from jax.experimental.pallas import tpu as pltpu
from jax.sharding import PartitionSpec as P

HEADS = 64
HEAD_DIM = 64
STATE_DIM = 128
GROUPS = 8
CONV_TAPS = 4
PER_GROUP = HEADS // GROUPS
GROUP_WIDTH = PER_GROUP * HEAD_DIM
LANES = 128
X_TILES = GROUP_WIDTH // LANES
SPAN = 512
RIM = 4
EXTRA = 16
F32 = jnp.float32
BF16 = jnp.bfloat16


def partner(place, slot):
    return place ^ slot


def swap(value, slot):
    return lax.ppermute(value, "tp", [(i, i ^ slot) for i in range(lax.axis_size("tp"))])


def from_behind(value, axis, steps):
    count = lax.axis_size(axis)
    return lax.ppermute(value, axis, [(i, i + steps) for i in range(count - steps)])


def in_three(value):
    high = value.astype(BF16).astype(F32)
    rest = value - high
    middle = rest.astype(BF16).astype(F32)
    low = rest - middle
    return jnp.concatenate([high, middle, low, jnp.zeros_like(value)], axis=0).astype(BF16)


def head_columns():
    rows = lax.broadcasted_iota(jnp.int32, (4 * PER_GROUP, GROUP_WIDTH), 0)
    columns = lax.broadcasted_iota(jnp.int32, (4 * PER_GROUP, GROUP_WIDTH), 1)
    own = lax.rem(rows, PER_GROUP) == lax.div(columns, HEAD_DIM)
    return jnp.where(own, 1.0, 0.0).astype(BF16)


def spread(value, columns):
    return lax.dot_general(
        in_three(value), columns, (((0,), (0,)), ((), ())), preferred_element_type=F32
    )


def column_of(ref, first, width=LANES):
    rows = lax.broadcasted_iota(jnp.int32, (PER_GROUP, width), 0)
    out = jnp.zeros((PER_GROUP, width), F32)
    for head in range(PER_GROUP):
        out = jnp.where(rows == head, ref[first + head], out)
    return out


def conv_tile(scratch, rim, rows, taps, shift):
    count = rows.shape[0]
    scratch[8 - RIM : 8, :] = rim.astype(F32)
    scratch[8 : 8 + count, :] = rows.astype(F32)
    total = shift + jnp.zeros((count, LANES), F32)
    for tap in range(CONV_TAPS):
        first = 8 - (CONV_TAPS - 1) + tap
        total = total + taps[tap : tap + 1, :] * scratch[first : first + count, :]
    return (total / (1.0 + jnp.exp(-total))).astype(BF16)


def send_kernel(group, tp, gd, x_ref, b_ref, dt_ref, rim_ref, tx_ref, sx_ref, tb_ref, sb_ref, *rest):
    outs, scratch = rest[:tp], rest[tp]
    rows = x_ref.shape[0]
    me = lax.axis_index("tp")
    eye_r = lax.broadcasted_iota(jnp.int32, (rows, rows), 0)
    eye_c = lax.broadcasted_iota(jnp.int32, (rows, rows), 1)
    eye = jnp.where(eye_r == eye_c, 1.0, 0.0).astype(BF16)
    steps = lax.dot_general(
        dt_ref[...], eye, (((0,), (0,)), ((), ())), preferred_element_type=F32
    )
    dt_scr = rest[tp + 1]
    dt_scr[...] = steps
    for slot in range(tp):
        out = outs[slot]
        whole = partner(me, slot) * gd + group
        for tile in range(X_TILES):
            at = pl.ds(pl.multiple_of(whole * GROUP_WIDTH + tile * LANES, LANES), LANES)
            out[tile * rows : (tile + 1) * rows, :] = conv_tile(
                scratch, rim_ref[:, at], x_ref[:, at], tx_ref[:, at], sx_ref[:, at]
            )
        at = pl.ds(pl.multiple_of(whole * STATE_DIM, LANES), LANES)
        width = x_ref.shape[1]
        rim_at = pl.ds(pl.multiple_of(width + whole * STATE_DIM, LANES), LANES)
        out[X_TILES * rows : (X_TILES + 1) * rows, :] = conv_tile(
            scratch, rim_ref[:, rim_at], b_ref[:, at], tb_ref[:, at], sb_ref[:, at]
        )
        mine = dt_scr[pl.ds(pl.multiple_of(whole * PER_GROUP, PER_GROUP), PER_GROUP), :]
        out[(X_TILES + 1) * rows :, :] = jnp.concatenate(
            [mine, jnp.zeros((EXTRA - PER_GROUP, rows), F32)], axis=0
        ).astype(BF16)


def last_send_kernel(tp, gd, kept, z_ref, c_ref, rim_ref, tc_ref, sc_ref, *rest):
    outs, scratch = rest[:tp], rest[tp]
    me = lax.axis_index("tp")
    gate_width = (gd - kept) * GROUP_WIDTH
    for slot in range(tp):
        out = outs[slot]
        place = partner(me, slot)
        at = pl.ds(
            pl.multiple_of(place * (gd * GROUP_WIDTH) + kept * GROUP_WIDTH, LANES), gate_width
        )
        out[:, :gate_width] = z_ref[:, at]
        for group in range(gd):
            first = (place * gd + group) * STATE_DIM
            at = pl.ds(pl.multiple_of(first, LANES), LANES)
            rim_at = pl.ds(
                pl.multiple_of(rim_ref.shape[1] - c_ref.shape[1] + first, LANES), LANES
            )
            out[:, gate_width + group * LANES : gate_width + (group + 1) * LANES] = conv_tile(
                scratch, rim_ref[:, rim_at], c_ref[:, at], tc_ref[:, at], sc_ref[:, at]
            )


def state_kernel(group, tp, spans, bias_ref, log_ref, *rest):
    pieces = rest[:tp]
    conv_ref, scaled_ref, b_ref, grow_ref, mid_ref, prior_ref, ship_ref = rest[tp : tp + 7]
    ahead_ref = rest[tp + 7] if spans > 1 else None
    step_scr = rest[-1]
    rows = conv_ref.shape[0] // tp
    per_span = tp // spans
    me = lax.axis_index("tp")
    for slot in range(tp):
        place = partner(me, slot)
        at = pl.ds(pl.multiple_of(place * rows, rows), rows)
        for tile in range(X_TILES):
            conv_ref[at, tile * LANES : (tile + 1) * LANES] = pieces[slot][
                tile * rows : (tile + 1) * rows, :
            ]
        b_ref[at, :] = pieces[slot][X_TILES * rows : (X_TILES + 1) * rows, :]
        step_scr[place] = pieces[slot][(X_TILES + 1) * rows :, :].astype(F32)[:PER_GROUP]
    bias = column_of(bias_ref, group * PER_GROUP, rows)
    rate = jnp.exp(column_of(log_ref, group * PER_GROUP, rows))
    steps, logs = [], []
    for place in range(tp):
        raw = step_scr[place] + bias
        step = jnp.maximum(raw, 0.0) + jnp.log1p(jnp.exp(-jnp.abs(raw)))
        steps.append(step)
        logs.append(-step * rate)
    tri_r = lax.broadcasted_iota(jnp.int32, (rows, rows), 0)
    tri_c = lax.broadcasted_iota(jnp.int32, (rows, rows), 1)
    tri = jnp.where(tri_r <= tri_c, 1.0, 0.0).astype(BF16)
    parts = jnp.dot(in_three(jnp.concatenate(logs, axis=0)), tri, preferred_element_type=F32)
    count = tp * PER_GROUP
    sums = parts[:count] + parts[count : 2 * count] + parts[2 * count : 3 * count]
    columns = head_columns()
    prior = jnp.zeros((PER_GROUP, rows), F32)
    total = None
    for span in range(spans):
        inside, running = [], jnp.zeros((PER_GROUP, rows), F32)
        for piece in range(per_span):
            first = (span * per_span + piece) * PER_GROUP
            local = sums[first : first + PER_GROUP]
            inside.append(running + local)
            running = running + jnp.broadcast_to(local[:, rows - 1 :], (PER_GROUP, rows))
            if piece == max(per_span // 2 - 1, 0):
                middle = running
        for piece in range(per_span):
            place = span * per_span + piece
            grow_ref[place] = jnp.exp(inside[piece] - middle)
            scale = spread(jnp.exp(middle - inside[piece]) * steps[place], columns)
            at = slice(place * rows, (place + 1) * rows)
            scaled_ref[at, :] = (conv_ref[at, :].astype(F32) * scale).astype(BF16)
        at = slice(span * per_span * rows, (span + 1) * per_span * rows)
        summed = lax.dot_general(
            b_ref[at, :], scaled_ref[at, :], (((0,), (0,)), ((), ())), preferred_element_type=F32
        )
        summed = summed * spread(jnp.exp(running - middle), columns)
        mid_ref[span] = middle
        prior_ref[span] = prior
        if spans > 1:
            ahead_ref[span] = total if total is not None else jnp.zeros_like(summed)
        total = summed if total is None else total * spread(jnp.exp(running), columns) + summed
        prior = prior + running
    ship_ref[:STATE_DIM, :] = total.astype(BF16)
    decay = spread(jnp.exp(prior), columns)[:EXTRA]
    high = decay.astype(BF16).astype(F32)
    middle = (decay - high).astype(BF16).astype(F32)
    at = lax.broadcasted_iota(jnp.int32, (EXTRA, GROUP_WIDTH), 0)
    stacked = jnp.where(at == 0, high, jnp.where(at == 1, middle, decay - high - middle))
    ship_ref[STATE_DIM:, :] = jnp.where(at < 3, stacked, 0.0).astype(BF16)


def shipped(ref):
    rows = ref[STATE_DIM:, :].astype(F32)
    return ref[:STATE_DIM, :].astype(F32), rows[0:1] + rows[1:2] + rows[2:3]


def out_kernel(group, tp, gd, kept, spans, states, skip_ref, gain_ref, *rest):
    early, late = rest[:tp], rest[tp : 2 * tp]
    rest = rest[2 * tp :]
    conv_ref, scaled_ref, b_ref, grow_ref, mid_ref, prior_ref = rest[:6]
    rest = rest[6:]
    ahead_ref = None
    if spans > 1:
        ahead_ref, rest = rest[0], rest[1:]
    sent, rest = rest[:states], rest[states:]
    if group > 0:
        rest = rest[1:]
    out_ref, start_scr = rest
    rows = late[0].shape[0]
    span_rows = tp // spans * rows
    me = lax.axis_index("tp")
    columns = head_columns()
    state = None
    for ref in reversed(sent):
        value, decay = shipped(ref)
        state = value if state is None else state * decay + value
    for span in range(spans):
        if spans == 1:
            start_scr[span] = (state * spread(jnp.exp(mid_ref[0]), columns)).astype(BF16)
        else:
            scale = spread(jnp.exp(prior_ref[span]), columns)
            start = state * scale + ahead_ref[span]
            start_scr[span] = (start * spread(jnp.exp(mid_ref[span]), columns)).astype(BF16)
    skip = spread(column_of(skip_ref, group * PER_GROUP), columns)[:1]
    gate_width = (gd - kept) * GROUP_WIDTH
    for slot in range(tp):
        place = partner(me, slot)
        span = lax.div(place, tp // spans)
        inside = pl.ds(pl.multiple_of(span * span_rows, span_rows), span_rows)
        at = pl.ds(pl.multiple_of(place * rows, rows), rows)
        c_tile = late[slot][:, gate_width + group * LANES : gate_width + (group + 1) * LANES]
        scores = lax.dot_general(
            c_tile, b_ref[inside, :], (((1,), (1,)), ((), ())), preferred_element_type=F32
        )
        t_at = lax.broadcasted_iota(jnp.int32, scores.shape, 0) + (place * rows - span * span_rows)
        s_at = lax.broadcasted_iota(jnp.int32, scores.shape, 1)
        masked = jnp.where(s_at <= t_at, scores, 0.0).astype(BF16)
        mixed = jnp.dot(masked, scaled_ref[inside, :], preferred_element_type=F32)
        mixed = mixed + jnp.dot(c_tile, start_scr[span], preferred_element_type=F32)
        mixed = mixed * spread(grow_ref[place], columns)
        mixed = mixed + skip * conv_ref[at, :].astype(F32)
        if group < kept:
            gate = early[slot][:, group * GROUP_WIDTH : (group + 1) * GROUP_WIDTH]
        else:
            first = (group - kept) * GROUP_WIDTH
            gate = late[slot][:, first : first + GROUP_WIDTH]
        gate = gate.astype(F32)
        gated = mixed * (gate / (1.0 + jnp.exp(-gate)))
        square = jnp.mean(gated * gated, axis=-1, keepdims=True)
        out_ref[at, :] = (gated * lax.rsqrt(square + 1e-5) * gain_ref[...]).astype(BF16)


def vmem(count):
    return [pl.BlockSpec(memory_space=pltpu.VMEM)] * count


def smem(count):
    return [pl.BlockSpec(memory_space=pltpu.SMEM)] * count


def call(kernel, ins, outs, scratch, scalars=0, name=None):
    return pl.pallas_call(
        kernel,
        in_specs=smem(scalars) + vmem(len(ins) - scalars),
        out_specs=vmem(len(outs)),
        out_shape=outs,
        scratch_shapes=scratch,
        name=name,
    )(*ins)


def scanned(ship):
    count = lax.axis_size("ctx")
    if count <= 4:
        return [from_behind(ship, "ctx", steps) for steps in range(1, count)]
    state = ship[:STATE_DIM].astype(F32)
    decay = jnp.sum(ship[STATE_DIM : STATE_DIM + 3].astype(F32), axis=0, keepdims=True)

    def packed(state, decay):
        high = decay.astype(BF16).astype(F32)
        middle = (decay - high).astype(BF16).astype(F32)
        rows = [state, high, middle, decay - high - middle]
        rows.append(jnp.zeros((EXTRA - 3, GROUP_WIDTH), F32))
        return jnp.concatenate(rows, axis=0).astype(BF16)

    steps = 1
    while steps < count:
        other = from_behind(packed(state, decay), "ctx", steps)
        state = other[:STATE_DIM].astype(F32) * decay + state
        decay = decay * jnp.sum(
            other[STATE_DIM : STATE_DIM + 3].astype(F32), axis=0, keepdims=True
        )
        steps *= 2
    return [from_behind(packed(state, decay), "ctx", 1)]


def shards(
    x_input, bc_input, z_input, dt_input, x_kernel, x_bias, bc_kernel, bc_bias, dt_bias, a_log,
    d_skip, norm_gain,
):
    tp = lax.axis_size("tp")
    me = lax.axis_index("tp")
    rows = x_input.shape[0]
    ctx_rows = rows * tp
    gd = GROUPS // tp
    spans = max(1, ctx_rows // SPAN)
    kept = gd // 2
    width = gd * GROUP_WIDTH
    shape = jax.ShapeDtypeStruct

    def trade(parts):
        return [parts[0]] + [swap(parts[slot], slot) for slot in range(1, tp)]

    early = []
    if kept:
        early = trade(
            [
                lax.dynamic_slice_in_dim(
                    z_input, partner(me, slot) * width, kept * GROUP_WIDTH, 1
                )
                for slot in range(tp)
            ]
        )
    b_input, c_input = bc_input[:, 0], bc_input[:, 1]
    tail = jnp.concatenate(
        [x_input[rows - RIM :], b_input[rows - RIM :], c_input[rows - RIM :]], axis=1
    )
    rim = from_behind(tail, ("ctx", "tp"), 1)
    x_shift = x_bias.reshape(1, -1)
    conv_scratch = pltpu.VMEM((8 + rows, LANES), F32)
    traded = []
    for group in range(gd):
        parts = call(
            functools.partial(send_kernel, group, tp, gd),
            [
                x_input, b_input, dt_input, rim, x_kernel, x_shift, bc_kernel[:, 0],
                bc_bias[0:1],
            ],
            [shape(((X_TILES + 1) * rows + EXTRA, LANES), BF16)] * tp,
            [conv_scratch, pltpu.VMEM((HEADS, rows), F32)],
            name=f"send{group}",
        )
        traded.append(trade(parts))
    late = trade(
        call(
            functools.partial(last_send_kernel, tp, gd, kept),
            [z_input, c_input, rim, bc_kernel[:, 1], bc_bias[1:2]],
            [shape((rows, (gd - kept) * GROUP_WIDTH + gd * LANES), BF16)] * tp,
            [conv_scratch],
            name="send_last",
        )
    )
    held = []
    for group in range(gd):
        outs = [
            shape((ctx_rows, GROUP_WIDTH), BF16),
            shape((ctx_rows, GROUP_WIDTH), BF16),
            shape((ctx_rows, STATE_DIM), BF16),
            shape((tp, PER_GROUP, rows), F32),
            shape((spans, PER_GROUP, rows), F32),
            shape((spans, PER_GROUP, rows), F32),
            shape((STATE_DIM + EXTRA, GROUP_WIDTH), BF16),
        ]
        if spans > 1:
            outs.append(shape((spans, STATE_DIM, GROUP_WIDTH), F32))
        made = call(
            functools.partial(state_kernel, group, tp, spans),
            [dt_bias, a_log] + traded[group],
            outs,
            [pltpu.VMEM((tp, PER_GROUP, rows), F32)],
            scalars=2,
            name=f"state{group}",
        )
        kept_values = list(made[:6]) + list(made[7:])
        held.append((kept_values, scanned(made[6])))
    gain = norm_gain.reshape(1, -1)
    out = None
    for group in range(gd):
        values, sent = held[group]
        ins = [d_skip, gain] + (early if kept else [late[0]] * tp) + late + values + sent
        aliases = {}
        specs = smem(1) + [pl.BlockSpec((1, GROUP_WIDTH), lambda i, g=group: (0, g))]
        specs += vmem(len(ins) - 2)
        if group > 0:
            aliases = {len(ins): 0}
            ins.append(out)
            specs.append(pl.BlockSpec(memory_space=pl.ANY))
        out = pl.pallas_call(
            functools.partial(out_kernel, group, tp, gd, kept, spans, len(sent)),
            grid=(1,),
            in_specs=specs,
            out_specs=pl.BlockSpec((ctx_rows, GROUP_WIDTH), lambda i, g=group: (0, g)),
            out_shape=shape((ctx_rows, width), BF16),
            scratch_shapes=[pltpu.VMEM((spans, STATE_DIM, GROUP_WIDTH), BF16)],
            input_output_aliases=aliases,
            name=f"out{group}",
        )(*ins)
    return out


def solution(mesh):
    lead = ("groups", "ctx", "tp")
    in_specs = (
        P(lead, None), P(lead, None, None), P(lead, None), P(lead, None), P(), P(), P(), P(),
        P("tp"), P("tp"), P("tp"), P("tp"),
    )
    out_specs = P(("groups", "ctx"), "tp")
    return jax.shard_map(shards, mesh=mesh, in_specs=in_specs, out_specs=out_specs, check_vma=False)
```

time: 142 us -> 75.7 us (0.53)
  the two profiles are of different devices: /device:TPU:0 before, /device:TPU:25 now
where the time goes in v1:
time: 75.7 us; the launch traced here: 75 us
  waiting for transfers between devices  23.2 us (31%)
  Pallas kernels  22.1 us (29%)
  starting transfers between devices  19.9 us (26%)
  local copies, waits for them, and re-layouts  9.45 us (12%)
    pallas_call x5, Pallas kernels, call(): pl.pallas_call(kernel, in_specs=smem(scalars) + vmem(len(ins) - scalars),...  13.8 us
    ppermute x7, waiting for transfers between devices, from_behind(): lax.ppermute(value, axis, [(i, i + steps) for i in range(count - steps)])  13.5 us
    ppermute x7, starting transfers between devices, from_behind(): lax.ppermute(value, axis, [(i, i + steps) for i in range(count - steps)])  11.4 us
    ppermute x12, waiting for transfers between devices, swap(): lax.ppermute(value, 'tp', [(i, i ^ slot) for i in range(lax.axis_size('tp...  9.66 us
    ppermute x12, starting transfers between devices, swap(): lax.ppermute(value, 'tp', [(i, i ^ slot) for i in range(lax.axis_size('tp...  8.43 us
    pallas_call x2, Pallas kernels, shards(): pl.pallas_call(functools.partial(out_kernel, group, tp, gd, kept, spans,...  8.34 us
    unnamed x49, local copies, waits for them, and re-layouts  3 us
    dynamic_slice x1, local copies, waits for them, and re-layouts, shards(): lax.dynamic_slice_in_dim(z_input, partner(me, slot) * width, kept * GROUP...  1.84 us
  transfers between devices with their start and end apart: 19, of which 4 were waited for; matrix products, arithmetic and copies ran while one was open for 7% of the time, Pallas kernels for 24%

profile of v1, /device:TPU:25, one launch (start us, length us, event | category | flops | bytes accessed | tf_op | source)
XLA Modules:
  0.0 75.0 jit_solution(17221923447779567878)
XLA Ops:
  0.0 0.8 %fusion.1 = (bf16[4,1,1024]{2,1,0:T(2,128)(2,1)S(1)}, bf16[4,1,1024]{2,1,0:T(2,128)(2,1)S(1)}) fusion(bf16[128,2,1024]{2,1,0:T(2,128)(2,1)} %param.13), kind=kLoop, calls=%fused_computation.12 | loop fusion | bytes 32768 | tf_op jit(solution)/shard_map/slice | solution.py:336
  0.8 0.9 %slice.38 = bf16[4,4096]{1,0:T(4,128)(2,1)S(1)} slice(bf16[128,4096]{1,0:T(8,128)(2,1)} %x_ref.3), slice={[124:128], [0:4096]} | slice | bytes 65536 | tf_op jit(solution)/shard_map/slice | solution.py:336
  1.7 3.7 %collective-permute-start.3 = (bf16[4,6144]{1,0:T(4,128)(2,1)S(1)}, bf16[4,6144]{1,0:T(4,128)(2,1)S(1)}, u32[]{:S(2)}, u32[]{:S(2)}) collective-permute-start(bf16[4,6144]{1,0:T(4,128)(2,1)S(1)} %pad_maximum_fusion), channel_id=1, source_target_pairs={{0,1},{1,2},{2,3},{3,4},{4,5},{5,6},{6,7},{7,8},{8,9},{9,10},{10,1... | collective-permute-start | bytes 147464 | tf_op jit(solution)/shard_map/ppermute | solution.py:36
  5.5 1.8 %constant_dynamic-slice_fusion = (bf16[128,512]{1,0:T(8,128)(2,1)S(1)}, bf16[128,512]{1,0:T(8,128)(2,1)S(1)}, bf16[128,512]{1,0:T(8,128)(2,1)S(1)}, bf16[128,512]{1,0:T(8,128)(2,1)}) fusion(bf16[128,4096]{1,0:T(8,128)(2,1)} %z_ref.1, s32[]{:T(128)S(6)} %select_n.15, s32[]{:T(128)S(6)} %select_n.14, s32[]{:T(128)S(6)} %select_n.13, s32[]{:T(128)S(6)} %select_n.12), kind=kLoop, calls=%fused_computation.7 | loop fusion | bytes 1048592 | tf_op jit(solution)/shard_map/dynamic_slice | solution.py:328
  7.4 2.0 %collective-permute-start.2 = (bf16[128,512]{1,0:T(8,128)(2,1)S(1)}, bf16[128,512]{1,0:T(8,128)(2,1)S(1)}, u32[]{:S(2)}, u32[]{:S(2)}) collective-permute-start(bf16[128,512]{1,0:T(8,128)(2,1)S(1)} %get-tuple-element.57), channel_id=1, source_target_pairs={{0,3},{1,2},{2,1},{3,0},{4,7},{5,6},{6,5},{7,4},{8,11},{9,10},{10,... | collective-permute-start | bytes 393224 | tf_op jit(solution)/shard_map/ppermute | solution.py:31
  9.4 0.7 fusion
  10.2 0.9 %copy_bitcast_fusion = (bf16[128,1024]{1,0:T(8,128)(2,1)}, bf16[128,1024]{1,0:T(8,128)(2,1)}) fusion(bf16[128,1,1024]{2,1,0:T(2,128)(2,1)S(1)} %get-tuple-element.61, bf16[128,1,1024]{2,1,0:T(2,128)(2,1)S(1)} %get-tuple-element.62), kind=kLoop, calls=%fused_computation | loop fusion | bytes 1048576 | tf_op jit(solution)/shard_map/squeeze | solution.py:334
  11.2 0.6 copy_bitcast_fusion.2
  12.6 0.7 copy.20.dt_ref
  13.3 0.6 copy-done.7
  13.9 3.0 %send0.1 = (bf16[656,128]{1,0:T(8,128)(2,1)}, bf16[656,128]{1,0:T(8,128)(2,1)}, bf16[656,128]{1,0:T(8,128)(2,1)}, bf16[656,128]{1,0:T(8,128)(2,1)}) custom-call(bf16[128,4096]{1,0:T(8,128)(2,1)} %x_ref.3, bf16[128,1024]{1,0:T(8,128)(2,1)} %get-tuple-element.69.b_ref, bf16[128,64]{1,0:T(8,128)(2,1)} %copy.20.dt_ref, bf16[4,6144]{1,0:T(4,128)(2,1)} %copy-done.7, ...), custom_call_target="tpu_custom_call" | custom-call | tf_op jit(solution)/shard_map/send0/pallas_call | solution.py:272
  17.0 2.0 %collective-permute-start.15 = (bf16[656,128]{1,0:T(8,128)(2,1)}, bf16[656,128]{1,0:T(8,128)(2,1)S(1)}, u32[]{:S(2)}, u32[]{:S(2)}) collective-permute-start(bf16[656,128]{1,0:T(8,128)(2,1)} %get-tuple-element.49), channel_id=1, source_target_pairs={{0,3},{1,2},{2,1},{3,0},{4,7},{5,6},{6,5},{7,4},{8,11},{9,10},{10,... | collective-permute-start | bytes 503816 | tf_op jit(solution)/shard_map/ppermute | solution.py:31
  19.0 3.0 %send1.1 = (bf16[656,128]{1,0:T(8,128)(2,1)}, bf16[656,128]{1,0:T(8,128)(2,1)}, bf16[656,128]{1,0:T(8,128)(2,1)}, bf16[656,128]{1,0:T(8,128)(2,1)}) custom-call(bf16[128,4096]{1,0:T(8,128)(2,1)} %x_ref.3, bf16[128,1024]{1,0:T(8,128)(2,1)} %get-tuple-element.69.b_ref, bf16[128,64]{1,0:T(8,128)(2,1)} %copy.20.dt_ref, bf16[4,6144]{1,0:T(4,128)(2,1)} %copy-done.7, ...), custom_call_target="tpu_custom_call" | custom-call | tf_op jit(solution)/shard_map/send1/pallas_call | solution.py:272
  22.2 2.4 %send_last.1 = (bf16[128,768]{1,0:T(8,128)(2,1)}, bf16[128,768]{1,0:T(8,128)(2,1)}, bf16[128,768]{1,0:T(8,128)(2,1)}, bf16[128,768]{1,0:T(8,128)(2,1)}) custom-call(bf16[128,4096]{1,0:T(8,128)(2,1)} %z_ref.1, bf16[128,1024]{1,0:T(8,128)(2,1)} %get-tuple-element.70.c_ref, bf16[4,6144]{1,0:T(4,128)(2,1)} %copy-done.7, f32[4,1024]{1,0:T(4,128)} %get-tuple-element.74.tc_ref, ...), custom_call_target="tpu_custom_call" | custom-call | tf_op jit(solution)/shard_map/send_last/pallas_call | solution.py:272
  25.2 1.7 %collective-permute-start.5 = (bf16[128,768]{1,0:T(8,128)(2,1)}, bf16[128,768]{1,0:T(8,128)(2,1)S(1)}, u32[]{:S(2)}, u32[]{:S(2)}) collective-permute-start(bf16[128,768]{1,0:T(8,128)(2,1)} %get-tuple-element.33), channel_id=1, source_target_pairs={{0,2},{1,3},{2,0},{3,1},{4,6},{5,7},{6,4},{7,5},{8,10},{9,11},{10,... | collective-permute-start | bytes 589832 | tf_op jit(solution)/shard_map/ppermute | solution.py:31
  26.9 0.8 %collective-permute-done.15.rest_3_ = bf16[656,128]{1,0:T(8,128)(2,1)S(1)} collective-permute-done((bf16[656,128]{1,0:T(8,128)(2,1)}, bf16[656,128]{1,0:T(8,128)(2,1)S(1)}, u32[]{:S(2)}, u32[]{:S(2)}) %collective-permute-start.15) | collective-permute-done | bytes 167968 | tf_op jit(solution)/shard_map/ppermute | solution.py:31
  27.7 1.8 %collective-permute-start.9 = (bf16[656,128]{1,0:T(8,128)(2,1)S(1)}, bf16[656,128]{1,0:T(8,128)(2,1)S(1)}, u32[]{:S(2)}, u32[]{:S(2)}) collective-permute-start(bf16[656,128]{1,0:T(8,128)(2,1)S(1)} %copy-done.23), channel_id=1, source_target_pairs={{0,3},{1,2},{2,1},{3,0},{4,7},{5,6},{6,5},{7,4},{8,11},{9,10},{10,... | collective-permute-start | bytes 503816 | tf_op jit(solution)/shard_map/ppermute | solution.py:31
  29.5 2.7 %state0.1 = (bf16[512,512]{1,0:T(8,128)(2,1)}, bf16[512,512]{1,0:T(8,128)(2,1)}, bf16[512,128]{1,0:T(8,128)(2,1)}, f32[4,8,128]{2,1,0:T(8,128)}, f32[1,8,128]{2,...) custom-call(f32[16]{0:T(128)} %bias_ref.3, f32[16]{0:T(128)} %log_ref.3, ...), custom_call_target="tpu_custom_call" | custom-call | tf_op jit(solution)/shard_map/state0/pallas_call | solution.py:272
  32.2 1.3 %collective-permute-start.16 = (bf16[144,512]{1,0:T(8,128)(2,1)}, bf16[144,512]{1,0:T(8,128)(2,1)S(1)}, u32[]{:S(2)}, u32[]{:S(2)}) collective-permute-start(bf16[144,512]{1,0:T(8,128)(2,1)} %get-tuple-element.56), channel_id=1, source_target_pairs={{0,4},{4,8},{8,12},{1,5},{5,9},{9,13},{2,6},{6,10},{10,14},{3,7},{... | collective-permute-start | bytes 442376 | tf_op jit(solution)/shard_map/ppermute | solution.py:36
  33.5 8.8 %collective-permute-done.9.rest_3_ = bf16[656,128]{1,0:T(8,128)(2,1)S(1)} collective-permute-done((bf16[656,128]{1,0:T(8,128)(2,1)S(1)}, bf16[656,128]{1,0:T(8,128)(2,1)S(1)}, u32[]{:S(2)}, u32[]{:S(2)}) %collective-permute-start.9) | collective-permute-done | bytes 167968 | tf_op jit(solution)/shard_map/ppermute | solution.py:31
  42.3 1.3 %collective-permute-start.17 = (bf16[144,512]{1,0:T(8,128)(2,1)}, bf16[144,512]{1,0:T(8,128)(2,1)S(1)}, u32[]{:S(2)}, u32[]{:S(2)}) collective-permute-start(bf16[144,512]{1,0:T(8,128)(2,1)} %get-tuple-element.56), channel_id=1, source_target_pairs={{0,8},{4,12},{1,9},{5,13},{2,10},{6,14},{3,11},{7,15},{16,24},{20,... | collective-permute-start | bytes 442376 | tf_op jit(solution)/shard_map/ppermute | solution.py:36
  43.6 1.3 %collective-permute-start.18 = (bf16[144,512]{1,0:T(8,128)(2,1)}, bf16[144,512]{1,0:T(8,128)(2,1)S(1)}, u32[]{:S(2)}, u32[]{:S(2)}) collective-permute-start(bf16[144,512]{1,0:T(8,128)(2,1)} %get-tuple-element.56), channel_id=1, source_target_pairs={{0,12},{1,13},{2,14},{3,15},{16,28},{17,29},{18,30},{19,31}} | collective-permute-start | bytes 442376 | tf_op jit(solution)/shard_map/ppermute | solution.py:36
  45.0 2.7 %state1.1 = (bf16[512,512]{1,0:T(8,128)(2,1)}, bf16[512,512]{1,0:T(8,128)(2,1)}, bf16[512,128]{1,0:T(8,128)(2,1)}, f32[4,8,128]{2,1,0:T(8,128)}, f32[1,8,128]{2,...) custom-call(f32[16]{0:T(128)} %bias_ref.3, f32[16]{0:T(128)} %log_ref.3, ...), custom_call_target="tpu_custom_call" | custom-call | tf_op jit(solution)/shard_map/state1/pallas_call | solution.py:272
  47.7 1.3 %collective-permute-start.10 = (bf16[144,512]{1,0:T(8,128)(2,1)}, bf16[144,512]{1,0:T(8,128)(2,1)S(1)}, u32[]{:S(2)}, u32[]{:S(2)}) collective-permute-start(bf16[144,512]{1,0:T(8,128)(2,1)} %get-tuple-element.45), channel_id=1, source_target_pairs={{0,4},{4,8},{8,12},{1,5},{5,9},{9,13},{2,6},{6,10},{10,14},{3,7},{... | collective-permute-start | bytes 442376 | tf_op jit(solution)/shard_map/ppermute | solution.py:36
  49.0 1.3 %collective-permute-start.11 = (bf16[144,512]{1,0:T(8,128)(2,1)}, bf16[144,512]{1,0:T(8,128)(2,1)S(1)}, u32[]{:S(2)}, u32[]{:S(2)}) collective-permute-start(bf16[144,512]{1,0:T(8,128)(2,1)} %get-tuple-element.45), channel_id=1, source_target_pairs={{0,8},{4,12},{1,9},{5,13},{2,10},{6,14},{3,11},{7,15},{16,24},{20,... | collective-permute-start | bytes 442376 | tf_op jit(solution)/shard_map/ppermute | solution.py:36
  50.4 1.3 %collective-permute-start.12 = (bf16[144,512]{1,0:T(8,128)(2,1)}, bf16[144,512]{1,0:T(8,128)(2,1)S(1)}, u32[]{:S(2)}, u32[]{:S(2)}) collective-permute-start(bf16[144,512]{1,0:T(8,128)(2,1)} %get-tuple-element.45), channel_id=1, source_target_pairs={{0,12},{1,13},{2,14},{3,15},{16,28},{17,29},{18,30},{19,31}} | collective-permute-start | bytes 442376 | tf_op jit(solution)/shard_map/ppermute | solution.py:36
  51.7 5.9 %collective-permute-done.17.rest_15_ = bf16[144,512]{1,0:T(8,128)(2,1)S(1)} collective-permute-done((bf16[144,512]{1,0:T(8,128)(2,1)}, bf16[144,512]{1,0:T(8,128)(2,1)S(1)}, u32[]{:S(2)}, u32[]{:S(2)}) %collective-permute-start.17) | collective-permute-done | bytes 147488 | tf_op jit(solution)/shard_map/ppermute | solution.py:36
  57.6 0.6 copy-done.15
  58.3 4.2 %out0.1.rest_17_ = bf16[512,1024]{1,0:T(8,128)(2,1)} custom-call(f32[16]{0:T(128)} %skip_ref.3, f32[1,1024]{1,0:T(1,128)} %bitcast.16, bf16[128,512]{1,0:T(8,128)(2,1)} %get-tuple-element.60.rest_0_, bf16[128,512]{1,0:T(8,128)(2,1)} %copy-done.4, bf16[128,512]{1,0:T(8,128)(2,1)} %copy-done.5, bf16[128,512]{1,0:T(8,128)(2,1)} %copy-done.6, ...), custom_call_target="tpu_custom_call" | custom-call | tf_op jit(solution)/shard_map/out0/pallas_call | solution.py:398
  62.5 7.6 %collective-permute-done.11.rest_15_ = bf16[144,512]{1,0:T(8,128)(2,1)S(1)} collective-permute-done((bf16[144,512]{1,0:T(8,128)(2,1)}, bf16[144,512]{1,0:T(8,128)(2,1)S(1)}, u32[]{:S(2)}, u32[]{:S(2)}) %collective-permute-start.11) | collective-permute-done | bytes 147488 | tf_op jit(solution)/shard_map/ppermute | solution.py:36
  70.1 0.6 copy-done.18
  70.8 4.2 %out1.1 = bf16[512,1024]{1,0:T(8,128)(2,1)} custom-call(f32[16]{0:T(128)} %skip_ref.3, f32[1,1024]{1,0:T(1,128)} %bitcast.17, bf16[128,512]{1,0:T(8,128)(2,1)} %get-tuple-element.60.rest_0_, bf16[128,512]{1,0:T(8,128)(2,1)} %copy-done.4, bf16[128,512]{1,0:T(8,128)(2,1)} %copy-done.5, bf16[128,512]{1,0:T(8,128)(2,1)} %copy-done.6, ...), custom_call_target="tpu_custom_call", output_to_operand_aliasing={{}: (19, {})} | custom-call | tf_op jit(solution)/shard_map/out1/pallas_call | solution.py:398
  (72 shorter events, 2.0 us)
Async XLA Ops:
  1.7 11.6 %collective-permute-start.3 = (bf16[4,6144]{1,0:T(4,128)(2,1)S(1)}, bf16[4,6144]{1,0:T(4,128)(2,1)S(1)}, u32[]{:S(2)}, u32[]{:S(2)}) collective-permute-start(bf16[4,6144]{1,0:T(4,128)(2,1)S(1)} %pad_maximum_fusion), channel_id=1, source_target_pairs={{0,1},{1,2},{2,3},{3,4},{4,5},{5,6},{6,7},{7,8},{8,9},{9,10},{10,1... | collective-permute-start | bytes 147464 | tf_op jit(solution)/shard_map/ppermute | solution.py:36
  5.5 4.0 %copy-start = (bf16[128,2,1024]{2,1,0:T(2,128)(2,1)S(1)}, bf16[128,2,1024]{2,1,0:T(2,128)(2,1)}, u32[]{:S(2)}) copy-start(bf16[128,2,1024]{2,1,0:T(2,128)(2,1)} %param.13) | copy-start | bytes 1572868
  7.3 9.7 %collective-permute-start = (bf16[128,512]{1,0:T(8,128)(2,1)S(1)}, bf16[128,512]{1,0:T(8,128)(2,1)S(1)}, u32[]{:S(2)}, u32[]{:S(2)}) collective-permute-start(bf16[128,512]{1,0:T(8,128)(2,1)S(1)} %get-tuple-element.59), channel_id=1, source_target_pairs={{0,1},{1,0},{2,3},{3,2},{4,5},{5,4},{6,7},{7,6},{8,9},{9,8},{10,11... | collective-permute-start | bytes 393224 | tf_op jit(solution)/shard_map/ppermute | solution.py:31
  7.3 14.7 %collective-permute-start.1 = (bf16[128,512]{1,0:T(8,128)(2,1)S(1)}, bf16[128,512]{1,0:T(8,128)(2,1)S(1)}, u32[]{:S(2)}, u32[]{:S(2)}) collective-permute-start(bf16[128,512]{1,0:T(8,128)(2,1)S(1)} %get-tuple-element.58), channel_id=1, source_target_pairs={{0,2},{1,3},{2,0},{3,1},{4,6},{5,7},{6,4},{7,5},{8,10},{9,11},{10,... | collective-permute-start | bytes 393224 | tf_op jit(solution)/shard_map/ppermute | solution.py:31
  7.4 2.8 %copy-start.20 = (f32[4,2,1024]{2,1,0:T(2,128)S(1)}, f32[4,2,1024]{2,1,0:T(2,128)}, u32[]{:S(2)}) copy-start(f32[4,2,1024]{2,1,0:T(2,128)} %param.18) | copy-start | bytes 98308
  7.4 14.7 %collective-permute-start.2 = (bf16[128,512]{1,0:T(8,128)(2,1)S(1)}, bf16[128,512]{1,0:T(8,128)(2,1)S(1)}, u32[]{:S(2)}, u32[]{:S(2)}) collective-permute-start(bf16[128,512]{1,0:T(8,128)(2,1)S(1)} %get-tuple-element.57), channel_id=1, source_target_pairs={{0,3},{1,2},{2,1},{3,0},{4,7},{5,6},{6,5},{7,4},{8,11},{9,10},{10,... | collective-permute-start | bytes 393224 | tf_op jit(solution)/shard_map/ppermute | solution.py:31
  16.9 7.8 %collective-permute-start.13 = (bf16[656,128]{1,0:T(8,128)(2,1)}, bf16[656,128]{1,0:T(8,128)(2,1)S(1)}, u32[]{:S(2)}, u32[]{:S(2)}) collective-permute-start(bf16[656,128]{1,0:T(8,128)(2,1)} %get-tuple-element.47), channel_id=1, source_target_pairs={{0,1},{1,0},{2,3},{3,2},{4,5},{5,4},{6,7},{7,6},{8,9},{9,8},{10,11... | collective-permute-start | bytes 503816 | tf_op jit(solution)/shard_map/ppermute | solution.py:31
  16.9 8.3 %collective-permute-start.14 = (bf16[656,128]{1,0:T(8,128)(2,1)}, bf16[656,128]{1,0:T(8,128)(2,1)S(1)}, u32[]{:S(2)}, u32[]{:S(2)}) collective-permute-start(bf16[656,128]{1,0:T(8,128)(2,1)} %get-tuple-element.48), channel_id=1, source_target_pairs={{0,2},{1,3},{2,0},{3,1},{4,6},{5,7},{6,4},{7,5},{8,10},{9,11},{10,... | collective-permute-start | bytes 503816 | tf_op jit(solution)/shard_map/ppermute | solution.py:31
  17.0 5.0 %copy-start.4 = (bf16[128,512]{1,0:T(8,128)(2,1)}, bf16[128,512]{1,0:T(8,128)(2,1)S(1)}, u32[]{:S(2)}) copy-start(bf16[128,512]{1,0:T(8,128)(2,1)S(1)} %collective-permute-done.rest_1_) | copy-start | bytes 393220
  17.0 10.7 %collective-permute-start.15 = (bf16[656,128]{1,0:T(8,128)(2,1)}, bf16[656,128]{1,0:T(8,128)(2,1)S(1)}, u32[]{:S(2)}, u32[]{:S(2)}) collective-permute-start(bf16[656,128]{1,0:T(8,128)(2,1)} %get-tuple-element.49), channel_id=1, source_target_pairs={{0,3},{1,2},{2,1},{3,0},{4,7},{5,6},{6,5},{7,4},{8,11},{9,10},{10,... | collective-permute-start | bytes 503816 | tf_op jit(solution)/shard_map/ppermute | solution.py:31
  22.0 5.7 %collective-permute-start.7 = (bf16[656,128]{1,0:T(8,128)(2,1)}, bf16[656,128]{1,0:T(8,128)(2,1)S(1)}, u32[]{:S(2)}, u32[]{:S(2)}) collective-permute-start(bf16[656,128]{1,0:T(8,128)(2,1)} %get-tuple-element.36), channel_id=1, source_target_pairs={{0,1},{1,0},{2,3},{3,2},{4,5},{5,4},{6,7},{7,6},{8,9},{9,8},{10,11... | collective-permute-start | bytes 503816 | tf_op jit(solution)/shard_map/ppermute | solution.py:31
  22.1 10.1 %collective-permute-start.8 = (bf16[656,128]{1,0:T(8,128)(2,1)}, bf16[656,128]{1,0:T(8,128)(2,1)S(1)}, u32[]{:S(2)}, u32[]{:S(2)}) collective-permute-start(bf16[656,128]{1,0:T(8,128)(2,1)} %get-tuple-element.37), channel_id=1, source_target_pairs={{0,2},{1,3},{2,0},{3,1},{4,6},{5,7},{6,4},{7,5},{8,10},{9,11},{10,... | collective-permute-start | bytes 503816 | tf_op jit(solution)/shard_map/ppermute | solution.py:31
  22.2 5.5 %copy-start.23 = (bf16[656,128]{1,0:T(8,128)(2,1)S(1)}, bf16[656,128]{1,0:T(8,128)(2,1)}, u32[]{:S(2)}) copy-start(bf16[656,128]{1,0:T(8,128)(2,1)} %get-tuple-element.38) | copy-start | bytes 503812
  24.7 4.8 %copy-start.10 = (bf16[656,128]{1,0:T(8,128)(2,1)}, bf16[656,128]{1,0:T(8,128)(2,1)S(1)}, u32[]{:S(2)}) copy-start(bf16[656,128]{1,0:T(8,128)(2,1)S(1)} %collective-permute-done.13.rest_1_) | copy-start | bytes 503812
  24.7 18.9 %collective-permute-start.4 = (bf16[128,768]{1,0:T(8,128)(2,1)}, bf16[128,768]{1,0:T(8,128)(2,1)S(1)}, u32[]{:S(2)}, u32[]{:S(2)}) collective-permute-start(bf16[128,768]{1,0:T(8,128)(2,1)} %get-tuple-element.32), channel_id=1, source_target_pairs={{0,1},{1,0},{2,3},{3,2},{4,5},{5,4},{6,7},{7,6},{8,9},{9,8},{10,11... | collective-permute-start | bytes 589832 | tf_op jit(solution)/shard_map/ppermute | solution.py:31
  25.2 4.3 %copy-start.11 = (bf16[656,128]{1,0:T(8,128)(2,1)}, bf16[656,128]{1,0:T(8,128)(2,1)S(1)}, u32[]{:S(2)}) copy-start(bf16[656,128]{1,0:T(8,128)(2,1)S(1)} %collective-permute-done.14.rest_2_) | copy-start | bytes 503812
  25.2 22.5 %collective-permute-start.5 = (bf16[128,768]{1,0:T(8,128)(2,1)}, bf16[128,768]{1,0:T(8,128)(2,1)S(1)}, u32[]{:S(2)}, u32[]{:S(2)}) collective-permute-start(bf16[128,768]{1,0:T(8,128)(2,1)} %get-tuple-element.33), channel_id=1, source_target_pairs={{0,2},{1,3},{2,0},{3,1},{4,6},{5,7},{6,4},{7,5},{8,10},{9,11},{10,... | collective-permute-start | bytes 589832 | tf_op jit(solution)/shard_map/ppermute | solution.py:31
  27.7 21.3 %collective-permute-start.6 = (bf16[128,768]{1,0:T(8,128)(2,1)}, bf16[128,768]{1,0:T(8,128)(2,1)S(1)}, u32[]{:S(2)}, u32[]{:S(2)}) collective-permute-start(bf16[128,768]{1,0:T(8,128)(2,1)} %get-tuple-element.34), channel_id=1, source_target_pairs={{0,3},{1,2},{2,1},{3,0},{4,7},{5,6},{6,5},{7,4},{8,11},{9,10},{10,... | collective-permute-start | bytes 589832 | tf_op jit(solution)/shard_map/ppermute | solution.py:31
  27.7 4.5 %copy-start.8 = (bf16[656,128]{1,0:T(8,128)(2,1)}, bf16[656,128]{1,0:T(8,128)(2,1)S(1)}, u32[]{:S(2)}) copy-start(bf16[656,128]{1,0:T(8,128)(2,1)S(1)} %collective-permute-done.7.rest_1_) | copy-start | bytes 503812
  27.7 14.6 %collective-permute-start.9 = (bf16[656,128]{1,0:T(8,128)(2,1)S(1)}, bf16[656,128]{1,0:T(8,128)(2,1)S(1)}, u32[]{:S(2)}, u32[]{:S(2)}) collective-permute-start(bf16[656,128]{1,0:T(8,128)(2,1)S(1)} %copy-done.23), channel_id=1, source_target_pairs={{0,3},{1,2},{2,1},{3,0},{4,7},{5,6},{6,5},{7,4},{8,11},{9,10},{10,... | collective-permute-start | bytes 503816 | tf_op jit(solution)/shard_map/ppermute | solution.py:31
  32.2 12.8 %copy-start.9 = (bf16[656,128]{1,0:T(8,128)(2,1)}, bf16[656,128]{1,0:T(8,128)(2,1)S(1)}, u32[]{:S(2)}) copy-start(bf16[656,128]{1,0:T(8,128)(2,1)S(1)} %collective-permute-done.8.rest_2_) | copy-start | bytes 503812
  32.2 18.1 %collective-permute-start.16 = (bf16[144,512]{1,0:T(8,128)(2,1)}, bf16[144,512]{1,0:T(8,128)(2,1)S(1)}, u32[]{:S(2)}, u32[]{:S(2)}) collective-permute-start(bf16[144,512]{1,0:T(8,128)(2,1)} %get-tuple-element.56), channel_id=1, source_target_pairs={{0,4},{4,8},{8,12},{1,5},{5,9},{9,13},{2,6},{6,10},{10,14},{3,7},{... | collective-permute-start | bytes 442376 | tf_op jit(solution)/shard_map/ppermute | solution.py:36
  42.3 15.2 %collective-permute-start.17 = (bf16[144,512]{1,0:T(8,128)(2,1)}, bf16[144,512]{1,0:T(8,128)(2,1)S(1)}, u32[]{:S(2)}, u32[]{:S(2)}) collective-permute-start(bf16[144,512]{1,0:T(8,128)(2,1)} %get-tuple-element.56), channel_id=1, source_target_pairs={{0,8},{4,12},{1,9},{5,13},{2,10},{6,14},{3,11},{7,15},{16,24},{20,... | collective-permute-start | bytes 442376 | tf_op jit(solution)/shard_map/ppermute | solution.py:36
  43.6 4.1 %copy-start.1 = (bf16[128,768]{1,0:T(8,128)(2,1)}, bf16[128,768]{1,0:T(8,128)(2,1)S(1)}, u32[]{:S(2)}) copy-start(bf16[128,768]{1,0:T(8,128)(2,1)S(1)} %collective-permute-done.4.rest_5_) | copy-start | bytes 589828
  43.6 13.9 %collective-permute-start.18 = (bf16[144,512]{1,0:T(8,128)(2,1)}, bf16[144,512]{1,0:T(8,128)(2,1)S(1)}, u32[]{:S(2)}, u32[]{:S(2)}) collective-permute-start(bf16[144,512]{1,0:T(8,128)(2,1)} %get-tuple-element.56), channel_id=1, source_target_pairs={{0,12},{1,13},{2,14},{3,15},{16,28},{17,29},{18,30},{19,31}} | collective-permute-start | bytes 442376 | tf_op jit(solution)/shard_map/ppermute | solution.py:36
  47.7 9.8 %copy-start.2 = (bf16[128,768]{1,0:T(8,128)(2,1)}, bf16[128,768]{1,0:T(8,128)(2,1)S(1)}, u32[]{:S(2)}) copy-start(bf16[128,768]{1,0:T(8,128)(2,1)S(1)} %collective-permute-done.5.rest_6_) | copy-start | bytes 589828
  47.7 14.7 %collective-permute-start.10 = (bf16[144,512]{1,0:T(8,128)(2,1)}, bf16[144,512]{1,0:T(8,128)(2,1)S(1)}, u32[]{:S(2)}, u32[]{:S(2)}) collective-permute-start(bf16[144,512]{1,0:T(8,128)(2,1)} %get-tuple-element.45), channel_id=1, source_target_pairs={{0,4},{4,8},{8,12},{1,5},{5,9},{9,13},{2,6},{6,10},{10,14},{3,7},{... | collective-permute-start | bytes 442376 | tf_op jit(solution)/shard_map/ppermute | solution.py:36
  49.0 8.5 %copy-start.3 = (bf16[128,768]{1,0:T(8,128)(2,1)}, bf16[128,768]{1,0:T(8,128)(2,1)S(1)}, u32[]{:S(2)}) copy-start(bf16[128,768]{1,0:T(8,128)(2,1)S(1)} %collective-permute-done.6.rest_7_) | copy-start | bytes 589828
  49.0 21.0 %collective-permute-start.11 = (bf16[144,512]{1,0:T(8,128)(2,1)}, bf16[144,512]{1,0:T(8,128)(2,1)S(1)}, u32[]{:S(2)}, u32[]{:S(2)}) collective-permute-start(bf16[144,512]{1,0:T(8,128)(2,1)} %get-tuple-element.45), channel_id=1, source_target_pairs={{0,8},{4,12},{1,9},{5,13},{2,10},{6,14},{3,11},{7,15},{16,24},{20,... | collective-permute-start | bytes 442376 | tf_op jit(solution)/shard_map/ppermute | solution.py:36
  50.4 7.2 %copy-start.14 = (bf16[144,512]{1,0:T(8,128)(2,1)}, bf16[144,512]{1,0:T(8,128)(2,1)S(1)}, u32[]{:S(2)}) copy-start(bf16[144,512]{1,0:T(8,128)(2,1)S(1)} %collective-permute-done.16.rest_14_) | copy-start | bytes 442372
  50.4 19.7 %collective-permute-start.12 = (bf16[144,512]{1,0:T(8,128)(2,1)}, bf16[144,512]{1,0:T(8,128)(2,1)S(1)}, u32[]{:S(2)}, u32[]{:S(2)}) collective-permute-start(bf16[144,512]{1,0:T(8,128)(2,1)} %get-tuple-element.45), channel_id=1, source_target_pairs={{0,12},{1,13},{2,14},{3,15},{16,28},{17,29},{18,30},{19,31}} | collective-permute-start | bytes 442376 | tf_op jit(solution)/shard_map/ppermute | solution.py:36
  62.4 7.6 %copy-start.16 = (bf16[144,512]{1,0:T(8,128)(2,1)}, bf16[144,512]{1,0:T(8,128)(2,1)S(1)}, u32[]{:S(2)}) copy-start(bf16[144,512]{1,0:T(8,128)(2,1)S(1)} %collective-permute-done.10.rest_14_) | copy-start | bytes 442372
  (11 other events, 14.5 us)

commit v2 on v1

--- a/solution.py
+++ b/solution.py
@@ -19,6 +19,9 @@
 SPAN = 512
 RIM = 4
 EXTRA = 16
+SHORT = pl.CostEstimate(flops=1, bytes_accessed=1, transcendentals=1)
+LONG = pl.CostEstimate(flops=10**12, bytes_accessed=10**9, transcendentals=1)
+ROOM = 12 * 2**20
 F32 = jnp.float32
 BF16 = jnp.bfloat16
 
@@ -76,18 +79,49 @@
     return (total / (1.0 + jnp.exp(-total))).astype(BF16)
 
 
-def send_kernel(group, tp, gd, x_ref, b_ref, dt_ref, rim_ref, tx_ref, sx_ref, tb_ref, sb_ref, *rest):
-    outs, scratch = rest[:tp], rest[tp]
+def rim_kernel(x_ref, bc_ref, out_ref):
+    width = x_ref.shape[1]
+    count = bc_ref.shape[2]
+    rows = bc_ref.shape[0]
+    out_ref[:, :width] = x_ref[x_ref.shape[0] - RIM :, :]
+    for tile in range(count // LANES):
+        at = slice(tile * LANES, (tile + 1) * LANES)
+        both = bc_ref[:, :, at].astype(F32)
+        for part in range(2):
+            first = width + part * count + tile * LANES
+            out_ref[:, first : first + LANES] = both[rows - RIM :, part, :].astype(BF16)
+
+
+def load_kernel(count, *refs):
+    sems = refs[-1]
+    copies = [
+        pltpu.make_async_copy(refs[place], refs[count + place], sems.at[place])
+        for place in range(count)
+    ]
+    for copy in copies:
+        copy.start()
+    for copy in copies:
+        copy.wait()
+
+
+def conv_tile_of(scratch, rim_ref, bc_ref, taps_ref, shift_ref, part, first):
+    at = pl.ds(pl.multiple_of(first, LANES), LANES)
+    count = bc_ref.shape[2]
+    rim_at = pl.ds(
+        pl.multiple_of(rim_ref.shape[1] - (2 - part) * count + first, LANES), LANES
+    )
+    rows = bc_ref[:, :, at].astype(F32)[:, part, :]
+    taps = taps_ref[:, :, at][:, part, :]
+    return conv_tile(scratch, rim_ref[:, rim_at], rows, taps, shift_ref[part : part + 1, at])
+
+
+def send_kernel(
+    group, tp, gd, x_ref, bc_ref, dt_ref, rim_ref, tx_ref, sx_ref, tb_ref, sb_ref, *rest
+):
+    outs, scratch, dt_scr = rest[:tp], rest[tp], rest[tp + 1]
     rows = x_ref.shape[0]
     me = lax.axis_index("tp")
-    eye_r = lax.broadcasted_iota(jnp.int32, (rows, rows), 0)
-    eye_c = lax.broadcasted_iota(jnp.int32, (rows, rows), 1)
-    eye = jnp.where(eye_r == eye_c, 1.0, 0.0).astype(BF16)
-    steps = lax.dot_general(
-        dt_ref[...], eye, (((0,), (0,)), ((), ())), preferred_element_type=F32
-    )
-    dt_scr = rest[tp + 1]
-    dt_scr[...] = steps
+    dt_scr[...] = dt_ref[...].astype(F32)
     for slot in range(tp):
         out = outs[slot]
         whole = partner(me, slot) * gd + group
@@ -96,38 +130,27 @@
             out[tile * rows : (tile + 1) * rows, :] = conv_tile(
                 scratch, rim_ref[:, at], x_ref[:, at], tx_ref[:, at], sx_ref[:, at]
             )
-        at = pl.ds(pl.multiple_of(whole * STATE_DIM, LANES), LANES)
-        width = x_ref.shape[1]
-        rim_at = pl.ds(pl.multiple_of(width + whole * STATE_DIM, LANES), LANES)
-        out[X_TILES * rows : (X_TILES + 1) * rows, :] = conv_tile(
-            scratch, rim_ref[:, rim_at], b_ref[:, at], tb_ref[:, at], sb_ref[:, at]
+        out[X_TILES * rows : (X_TILES + 1) * rows, :] = conv_tile_of(
+            scratch, rim_ref, bc_ref, tb_ref, sb_ref, 0, whole * STATE_DIM
         )
         mine = dt_scr[pl.ds(pl.multiple_of(whole * PER_GROUP, PER_GROUP), PER_GROUP), :]
-        out[(X_TILES + 1) * rows :, :] = jnp.concatenate(
+        first = (X_TILES + 1) * rows
+        out[first : first + EXTRA, :] = jnp.concatenate(
             [mine, jnp.zeros((EXTRA - PER_GROUP, rows), F32)], axis=0
         ).astype(BF16)
-
-
-def last_send_kernel(tp, gd, kept, z_ref, c_ref, rim_ref, tc_ref, sc_ref, *rest):
-    outs, scratch = rest[:tp], rest[tp]
-    me = lax.axis_index("tp")
-    gate_width = (gd - kept) * GROUP_WIDTH
-    for slot in range(tp):
-        out = outs[slot]
-        place = partner(me, slot)
-        at = pl.ds(
-            pl.multiple_of(place * (gd * GROUP_WIDTH) + kept * GROUP_WIDTH, LANES), gate_width
-        )
-        out[:, :gate_width] = z_ref[:, at]
-        for group in range(gd):
-            first = (place * gd + group) * STATE_DIM
-            at = pl.ds(pl.multiple_of(first, LANES), LANES)
-            rim_at = pl.ds(
-                pl.multiple_of(rim_ref.shape[1] - c_ref.shape[1] + first, LANES), LANES
-            )
-            out[:, gate_width + group * LANES : gate_width + (group + 1) * LANES] = conv_tile(
-                scratch, rim_ref[:, rim_at], c_ref[:, at], tc_ref[:, at], sc_ref[:, at]
-            )
+        if group == gd - 1:
+            for other in range(gd):
+                first = (X_TILES + 1 + other) * rows + EXTRA
+                out[first : first + rows, :] = conv_tile_of(
+                    scratch, rim_ref, bc_ref, tb_ref, sb_ref, 1,
+                    (partner(me, slot) * gd + other) * STATE_DIM,
+                )
+
+
+def gate_kernel(z_ref, out_ref):
+    tp, _, width = out_ref.shape
+    for place in range(tp):
+        out_ref[place] = z_ref[:, place * width : (place + 1) * width]
 
 
 def state_kernel(group, tp, spans, bias_ref, log_ref, *rest):
@@ -146,7 +169,8 @@
                 tile * rows : (tile + 1) * rows, :
             ]
         b_ref[at, :] = pieces[slot][X_TILES * rows : (X_TILES + 1) * rows, :]
-        step_scr[place] = pieces[slot][(X_TILES + 1) * rows :, :].astype(F32)[:PER_GROUP]
+        first = (X_TILES + 1) * rows
+        step_scr[place] = pieces[slot][first : first + EXTRA, :].astype(F32)[:PER_GROUP]
     bias = column_of(bias_ref, group * PER_GROUP, rows)
     rate = jnp.exp(column_of(log_ref, group * PER_GROUP, rows))
     steps, logs = [], []
@@ -204,60 +228,80 @@
     return ref[:STATE_DIM, :].astype(F32), rows[0:1] + rows[1:2] + rows[2:3]
 
 
-def out_kernel(group, tp, gd, kept, spans, states, skip_ref, gain_ref, *rest):
-    early, late = rest[:tp], rest[tp : 2 * tp]
-    rest = rest[2 * tp :]
-    conv_ref, scaled_ref, b_ref, grow_ref, mid_ref, prior_ref = rest[:6]
-    rest = rest[6:]
+def mix_kernel(gd, spans, tp, skip_ref, *rest):
+    pieces, rest = rest[:tp], rest[tp:]
+    held, outs = rest[: 4 * gd], rest[4 * gd :]
+    rows = outs[0].shape[0] // tp
+    per_span = tp // spans
+    join = 2 if per_span % 2 == 0 else 1
+    me = lax.axis_index("tp")
+    columns = head_columns()
+    for group in range(gd):
+        conv_ref, scaled_ref, b_ref, grow_ref = held[4 * group : 4 * group + 4]
+        c_ref, mixed_ref = outs[2 * group : 2 * group + 2]
+        first = (X_TILES + 1 + group) * rows + EXTRA
+        for slot in range(tp):
+            at = pl.ds(pl.multiple_of(partner(me, slot) * rows, rows), rows)
+            c_ref[at, :] = pieces[slot][first : first + rows, :]
+        skip = spread(column_of(skip_ref, group * PER_GROUP), columns)[:1]
+        for place in range(0, tp, join):
+            span = place // per_span
+            at = slice(place * rows, (place + join) * rows)
+            inside = slice(span * per_span * rows, (place + join) * rows)
+            scores = lax.dot_general(
+                c_ref[at, :], b_ref[inside, :], (((1,), (1,)), ((), ())),
+                preferred_element_type=F32,
+            )
+            t_at = lax.broadcasted_iota(jnp.int32, scores.shape, 0)
+            s_at = lax.broadcasted_iota(jnp.int32, scores.shape, 1) - (at.start - inside.start)
+            masked = jnp.where(s_at <= t_at, scores, 0.0).astype(BF16)
+            mixed = jnp.dot(masked, scaled_ref[inside, :], preferred_element_type=F32)
+            grow = [spread(grow_ref[other], columns) for other in range(place, place + join)]
+            mixed = mixed * jnp.concatenate(grow, axis=0)
+            mixed_ref[at, :] = mixed + skip * conv_ref[at, :].astype(F32)
+
+
+def out_kernel(group, spans, states, gain_ref, gate_ref, c_ref, mixed_ref, grow_ref, *rest):
+    mid_ref, prior_ref = rest[:2]
+    rest = rest[2:]
     ahead_ref = None
     if spans > 1:
         ahead_ref, rest = rest[0], rest[1:]
     sent, rest = rest[:states], rest[states:]
-    if group > 0:
-        rest = rest[1:]
-    out_ref, start_scr = rest
-    rows = late[0].shape[0]
-    span_rows = tp // spans * rows
-    me = lax.axis_index("tp")
+    out_ref = rest[-1]
+    tp, rows, _ = gate_ref.shape
+    per_span = tp // spans
     columns = head_columns()
     state = None
     for ref in reversed(sent):
         value, decay = shipped(ref)
         state = value if state is None else state * decay + value
+    join = 2 if per_span % 2 == 0 else 1
     for span in range(spans):
-        if spans == 1:
-            start_scr[span] = (state * spread(jnp.exp(mid_ref[0]), columns)).astype(BF16)
-        else:
-            scale = spread(jnp.exp(prior_ref[span]), columns)
-            start = state * scale + ahead_ref[span]
-            start_scr[span] = (start * spread(jnp.exp(mid_ref[span]), columns)).astype(BF16)
-    skip = spread(column_of(skip_ref, group * PER_GROUP), columns)[:1]
-    gate_width = (gd - kept) * GROUP_WIDTH
-    for slot in range(tp):
-        place = partner(me, slot)
-        span = lax.div(place, tp // spans)
-        inside = pl.ds(pl.multiple_of(span * span_rows, span_rows), span_rows)
-        at = pl.ds(pl.multiple_of(place * rows, rows), rows)
-        c_tile = late[slot][:, gate_width + group * LANES : gate_width + (group + 1) * LANES]
-        scores = lax.dot_general(
-            c_tile, b_ref[inside, :], (((1,), (1,)), ((), ())), preferred_element_type=F32
-        )
-        t_at = lax.broadcasted_iota(jnp.int32, scores.shape, 0) + (place * rows - span * span_rows)
-        s_at = lax.broadcasted_iota(jnp.int32, scores.shape, 1)
-        masked = jnp.where(s_at <= t_at, scores, 0.0).astype(BF16)
-        mixed = jnp.dot(masked, scaled_ref[inside, :], preferred_element_type=F32)
-        mixed = mixed + jnp.dot(c_tile, start_scr[span], preferred_element_type=F32)
-        mixed = mixed * spread(grow_ref[place], columns)
-        mixed = mixed + skip * conv_ref[at, :].astype(F32)
-        if group < kept:
-            gate = early[slot][:, group * GROUP_WIDTH : (group + 1) * GROUP_WIDTH]
-        else:
-            first = (group - kept) * GROUP_WIDTH
-            gate = late[slot][:, first : first + GROUP_WIDTH]
-        gate = gate.astype(F32)
-        gated = mixed * (gate / (1.0 + jnp.exp(-gate)))
-        square = jnp.mean(gated * gated, axis=-1, keepdims=True)
-        out_ref[at, :] = (gated * lax.rsqrt(square + 1e-5) * gain_ref[...]).astype(BF16)
+        start = state
+        if spans > 1:
+            start = start * spread(jnp.exp(prior_ref[span]), columns) + ahead_ref[span]
+        start = (start * spread(jnp.exp(mid_ref[span]), columns)).astype(BF16)
+        for first in range(span * per_span, (span + 1) * per_span, join):
+            tall = join * rows
+            at = slice(first * rows, first * rows + tall)
+            carried = jnp.dot(c_ref[at, :], start, preferred_element_type=F32)
+            grow = [spread(grow_ref[place], columns) for place in range(first, first + join)]
+            mixed = mixed_ref[at, :] + carried * jnp.concatenate(grow, axis=0)
+            z_at = group * GROUP_WIDTH
+            gate = gate_ref[first : first + join, :, z_at : z_at + GROUP_WIDTH]
+            gate = gate.reshape(tall, GROUP_WIDTH).astype(F32)
+            gated = mixed * (gate / (1.0 + jnp.exp(-gate)))
+            square = jnp.mean(gated * gated, axis=-1, keepdims=True)
+            out_ref[at, :] = (gated * lax.rsqrt(square + 1e-5) * gain_ref[...]).astype(BF16)
+
+
+def close(value):
+    return pltpu.with_memory_space_constraint(value, pltpu.VMEM)
+
+
+def far(value):
+    return pltpu.with_memory_space_constraint(value, pltpu.HBM)
 
 
 def vmem(count):
@@ -268,13 +312,17 @@
     return [pl.BlockSpec(memory_space=pltpu.SMEM)] * count
 
 
-def call(kernel, ins, outs, scratch, scalars=0, name=None):
+def call(kernel, ins, outs, scratch, scalars=0, near=(), cost=LONG, name=None):
+    ins = [close(value) if place in near else value for place, value in enumerate(ins)]
+    outs = [pltpu.VMEM(out.shape, out.dtype) for out in outs]
     return pl.pallas_call(
         kernel,
         in_specs=smem(scalars) + vmem(len(ins) - scalars),
         out_specs=vmem(len(outs)),
         out_shape=outs,
         scratch_shapes=scratch,
+        compiler_params=pltpu.CompilerParams(vmem_limit_bytes=ROOM),
+        cost_estimate=cost,
         name=name,
     )(*ins)
 
@@ -309,57 +357,65 @@
     d_skip, norm_gain,
 ):
     tp = lax.axis_size("tp")
-    me = lax.axis_index("tp")
     rows = x_input.shape[0]
     ctx_rows = rows * tp
     gd = GROUPS // tp
     spans = max(1, ctx_rows // SPAN)
-    kept = gd // 2
     width = gd * GROUP_WIDTH
     shape = jax.ShapeDtypeStruct
 
     def trade(parts):
         return [parts[0]] + [swap(parts[slot], slot) for slot in range(1, tp)]
 
-    early = []
-    if kept:
-        early = trade(
-            [
-                lax.dynamic_slice_in_dim(
-                    z_input, partner(me, slot) * width, kept * GROUP_WIDTH, 1
-                )
-                for slot in range(tp)
-            ]
-        )
-    b_input, c_input = bc_input[:, 0], bc_input[:, 1]
-    tail = jnp.concatenate(
-        [x_input[rows - RIM :], b_input[rows - RIM :], c_input[rows - RIM :]], axis=1
-    )
+    count = bc_input.shape[2]
+    every = x_input.shape[1] + 2 * count
+    tail = pl.pallas_call(
+        rim_kernel,
+        grid=(1,),
+        in_specs=[
+            pl.BlockSpec((16, x_input.shape[1]), lambda i: (rows // 16 - 1, 0)),
+            pl.BlockSpec((8, 2, count), lambda i: (rows // 8 - 1, 0, 0)),
+        ],
+        out_specs=pl.BlockSpec((RIM, every), lambda i: (0, 0)),
+        out_shape=shape((RIM, every), BF16),
+        compiler_params=pltpu.CompilerParams(vmem_limit_bytes=ROOM),
+        name="rim",
+    )(far(x_input), far(bc_input))
     rim = from_behind(tail, ("ctx", "tp"), 1)
-    x_shift = x_bias.reshape(1, -1)
+    used = [
+        far(value)
+        for value in (
+            x_input, bc_input, dt_input.T, x_kernel, x_bias.reshape(1, -1), bc_kernel, bc_bias
+        )
+    ]
+    x_near, bc_near, *others = pl.pallas_call(
+        functools.partial(load_kernel, len(used)),
+        in_specs=[pl.BlockSpec(memory_space=pltpu.HBM)] * len(used),
+        out_specs=vmem(len(used)),
+        out_shape=[pltpu.VMEM(value.shape, value.dtype) for value in used],
+        scratch_shapes=[pltpu.SemaphoreType.DMA((len(used),))],
+        compiler_params=pltpu.CompilerParams(vmem_limit_bytes=ROOM),
+        cost_estimate=LONG,
+        name="load",
+    )(*used)
     conv_scratch = pltpu.VMEM((8 + rows, LANES), F32)
+    gates = call(
+        gate_kernel, [z_input], [shape((tp, rows, width), BF16)], [], cost=SHORT, name="gates"
+    )[0]
     traded = []
     for group in range(gd):
+        tall = (X_TILES + 1 + (gd if group == gd - 1 else 0)) * rows + EXTRA
         parts = call(
             functools.partial(send_kernel, group, tp, gd),
-            [
-                x_input, b_input, dt_input, rim, x_kernel, x_shift, bc_kernel[:, 0],
-                bc_bias[0:1],
-            ],
-            [shape(((X_TILES + 1) * rows + EXTRA, LANES), BF16)] * tp,
+            [x_near, bc_near, others[0], rim] + others[1:],
+            [shape((tall, LANES), BF16)] * tp,
             [conv_scratch, pltpu.VMEM((HEADS, rows), F32)],
+            near=range(8),
             name=f"send{group}",
         )
+        rim, parts = lax.optimization_barrier((rim, parts))
         traded.append(trade(parts))
-    late = trade(
-        call(
-            functools.partial(last_send_kernel, tp, gd, kept),
-            [z_input, c_input, rim, bc_kernel[:, 1], bc_bias[1:2]],
-            [shape((rows, (gd - kept) * GROUP_WIDTH + gd * LANES), BF16)] * tp,
-            [conv_scratch],
-            name="send_last",
-        )
-    )
+    gates, traded[-1][1] = lax.optimization_barrier((gates, traded[-1][1]))
     held = []
     for group in range(gd):
         outs = [
@@ -379,30 +435,49 @@
             outs,
             [pltpu.VMEM((tp, PER_GROUP, rows), F32)],
             scalars=2,
+            near=range(2, 2 + tp),
+            cost=LONG if group == 0 else SHORT,
             name=f"state{group}",
         )
+        ship = made[6]
         kept_values = list(made[:6]) + list(made[7:])
-        held.append((kept_values, scanned(made[6])))
+        held.append((kept_values, scanned(ship)))
+    gates = lax.all_to_all(gates, "tp", split_axis=0, concat_axis=0, tiled=True)
     gain = norm_gain.reshape(1, -1)
+    ins = [d_skip] + traded[-1]
+    for values, _ in held:
+        ins += values[:4]
+    mixed = call(
+        functools.partial(mix_kernel, gd, spans, tp),
+        ins,
+        [shape((ctx_rows, STATE_DIM), BF16), shape((ctx_rows, GROUP_WIDTH), F32)] * gd,
+        [],
+        scalars=1,
+        near=range(1, len(ins)),
+        cost=SHORT,
+        name="mix",
+    )
     out = None
     for group in range(gd):
         values, sent = held[group]
-        ins = [d_skip, gain] + (early if kept else [late[0]] * tp) + late + values + sent
+        ins = [gates, mixed[2 * group], mixed[2 * group + 1]] + values[3:] + sent
+        ins = [gain] + [close(value) for value in ins]
         aliases = {}
-        specs = smem(1) + [pl.BlockSpec((1, GROUP_WIDTH), lambda i, g=group: (0, g))]
-        specs += vmem(len(ins) - 2)
+        specs = [pl.BlockSpec((1, GROUP_WIDTH), lambda i, g=group: (0, g))]
+        specs += vmem(len(ins) - 1)
         if group > 0:
             aliases = {len(ins): 0}
             ins.append(out)
             specs.append(pl.BlockSpec(memory_space=pl.ANY))
         out = pl.pallas_call(
-            functools.partial(out_kernel, group, tp, gd, kept, spans, len(sent)),
+            functools.partial(out_kernel, group, spans, len(sent)),
             grid=(1,),
             in_specs=specs,
             out_specs=pl.BlockSpec((ctx_rows, GROUP_WIDTH), lambda i, g=group: (0, g)),
             out_shape=shape((ctx_rows, width), BF16),
-            scratch_shapes=[pltpu.VMEM((spans, STATE_DIM, GROUP_WIDTH), BF16)],
             input_output_aliases=aliases,
+            compiler_params=pltpu.CompilerParams(vmem_limit_bytes=ROOM),
+            cost_estimate=LONG,
             name=f"out{group}",
         )(*ins)
     return out

time: 75.7 us -> 59.9 us (0.79)
  waiting for transfers between devices: 23.2 us -> 13.9 us
  local copies, waits for them, and re-layouts: 9.45 us -> 1.38 us
  starting transfers between devices: 19.9 us -> 21.8 us
    ppermute x7, waiting for transfers between devices: 13.5 us -> 8.14 us  [from_behind(): lax.ppermute(value, axis, [(i, i + steps) for i in range(count - steps)])]
    all_to_all x0 -> x1, starting transfers between devices: none -> 4.71 us  [shards(): gates = lax.all_to_all(gates, 'tp', split_axis=0, concat_axis=0, tiled=True)]
    ppermute x12 -> x6, waiting for transfers between devices: 9.66 us -> 5.73 us  [swap(): lax.ppermute(value, 'tp', [(i, i ^ slot) for i in range(lax.axis_size('tp...]
    slice x6 -> x0, local copies, waits for them, and re-layouts: 3.05 us -> none  [the longest x1 0.86 us: shards(): x_input[rows - RIM:]]
    ppermute x12 -> x6, starting transfers between devices: 8.43 us -> 5.64 us  [swap(): lax.ppermute(value, 'tp', [(i, i ^ slot) for i in range(lax.axis_size('tp...]
    dynamic_slice x1 -> x0, local copies, waits for them, and re-layouts: 1.84 us -> none  [shards(): lax.dynamic_slice_in_dim(z_input, partner(me, slot) * width, kept * GROUP...]
    unnamed x49 -> x18, local copies, waits for them, and re-layouts: 3 us -> 1.38 us
    squeeze x2 -> x0, local copies, waits for them, and re-layouts: 1.56 us -> none  [the longest x1 0.95 us: shards(): b_input, c_input = (bc_input[:, 0], bc_input[:, 1])]
  transfers between devices with their start and end apart: 19 -> 14, of which waited for: 4 -> 3; matrix products, arithmetic and copies ran while one was open for 7% -> 0% of each run, Pallas kernels for 24% -> 20%
where the time goes in v2:
time: 59.9 us; the launch traced here: 59.4 us
  Pallas kernels  22.2 us (37%)
  starting transfers between devices  21.8 us (36%)
  waiting for transfers between devices  13.9 us (23%)
  local copies, waits for them, and re-layouts  1.38 us (2%)
    pallas_call x6, Pallas kernels, call(): pl.pallas_call(kernel, in_specs=smem(scalars) + vmem(len(ins) - scalars),...  13.1 us
    ppermute x7, starting transfers between devices, from_behind(): lax.ppermute(value, axis, [(i, i + steps) for i in range(count - steps)])  11.4 us
    ppermute x7, waiting for transfers between devices, from_behind(): lax.ppermute(value, axis, [(i, i + steps) for i in range(count - steps)])  8.14 us
    pallas_call x2, Pallas kernels, shards(): pl.pallas_call(functools.partial(out_kernel, group, spans, len(sent)), gr...  6.09 us
    ppermute x6, waiting for transfers between devices, swap(): lax.ppermute(value, 'tp', [(i, i ^ slot) for i in range(lax.axis_size('tp...  5.73 us
    ppermute x6, starting transfers between devices, swap(): lax.ppermute(value, 'tp', [(i, i ^ slot) for i in range(lax.axis_size('tp...  5.64 us
    all_to_all x1, starting transfers between devices, shards(): gates = lax.all_to_all(gates, 'tp', split_axis=0, concat_axis=0, tiled=True)  4.71 us
    pallas_call x1, Pallas kernels, shards(): pl.pallas_call(rim_kernel, grid=(1,), in_specs=[pl.BlockSpec((16, x_input...  1.56 us
  transfers between devices with their start and end apart: 14, of which 3 were waited for; matrix products, arithmetic and copies ran while one was open for 0% of the time, Pallas kernels for 20%

profile of v2, /device:TPU:25, one launch (start us, length us, event | category | flops | bytes accessed | tf_op | source)
XLA Modules:
  0.0 59.4 jit_solution(17458706997161155901)
XLA Ops:
  0.0 1.6 %rim.1 = bf16[4,6144]{1,0:T(4,128)(2,1)} custom-call(bf16[128,4096]{1,0:T(8,128)(2,1)} %refs_0_.1, bf16[128,2,1024]{2,1,0:T(2,128)(2,1)} %refs_1_.1), custom_call_target="tpu_custom_call" | custom-call | tf_op jit(solution)/shard_map/rim/pallas_call | solution.py:372
  1.6 3.7 %collective-permute-start = (bf16[4,6144]{1,0:T(4,128)(2,1)}, bf16[4,6144]{1,0:T(4,128)(2,1)}, u32[]{:S(2)}, u32[]{:S(2)}) collective-permute-start(bf16[4,6144]{1,0:T(4,128)(2,1)} %rim.1), channel_id=1, source_target_pairs={{0,1},{1,2},{2,3},{3,4},{4,5},{5,6},{6,7},{7,8},{8,9},{9,10},{10,1... | collective-permute-start | bytes 147464 | tf_op jit(solution)/shard_map/ppermute | solution.py:39
  5.2 1.4 %load.1 = (bf16[128,4096]{1,0:T(8,128)(2,1)S(1)}, bf16[128,2,1024]{2,1,0:T(2,128)(2,1)S(1)}, bf16[64,128]{1,0:T(8,128)(2,1)S(1)}, f32[4,4096]{1,0:T(4,128)S(1)},...) custom-call(bf16[128,4096]{1,0:T(8,128)(2,1)} %refs_0_.1, bf16[128,2,1024]{2,1,0:T(2,128)(2,1)} %refs_1_.1, ...), custom_call_target="tpu_custom_call" | custom-call | flops 999999995904 | bytes 1000000000 | tf_op jit(solution)/shard_map/load/pallas_call | solution.py:391
  6.7 0.0 collective-permute-done.rim_ref
  6.7 1.9 %send0.1 = (bf16[656,128]{1,0:T(8,128)(2,1)S(1)}, bf16[656,128]{1,0:T(8,128)(2,1)S(1)}, bf16[656,128]{1,0:T(8,128)(2,1)S(1)}, bf16[656,128]{1,0:T(8,128)(2,1)S(1)}) custom-call(bf16[128,4096]{1,0:T(8,128)(2,1)S(1)} %get-tuple-element.49.x_ref, bf16[128,2,1024]{2,1,0:T(2,128)(2,1)S(1)} %get-tuple-element.50.bc_ref, ...), custom_call_target="tpu_custom_call" | custom-call | flops 999999995904 | bytes 1000000000 | tf_op jit(solution)/shard_map/send0/pallas_call | solution.py:318
  8.7 0.0 copy-start
  8.7 3.7 %send1.1 = (bf16[912,128]{1,0:T(8,128)(2,1)S(1)}, bf16[912,128]{1,0:T(8,128)(2,1)S(1)}, bf16[912,128]{1,0:T(8,128)(2,1)}, bf16[912,128]{1,0:T(8,128)(2,1)}) custom-call(bf16[128,4096]{1,0:T(8,128)(2,1)S(1)} %get-tuple-element.49.x_ref, bf16[128,2,1024]{2,1,0:T(2,128)(2,1)S(1)} %get-tuple-element.50.bc_ref, bf16[64,128]{1,0:T(8,128)(2,1)S(1)} %get-tuple-element.51.dt_ref, ...), custom_call_target="tpu_custom_call" | custom-call | flops 999999995904 | bytes 1000000000 | tf_op jit(solution)/shard_map/send1/pallas_call | solution.py:318
  12.3 2.1 %collective-permute-start.1 = (bf16[912,128]{1,0:T(8,128)(2,1)S(1)}, bf16[912,128]{1,0:T(8,128)(2,1)S(1)}, u32[]{:S(2)}, u32[]{:S(2)}) collective-permute-start(bf16[912,128]{1,0:T(8,128)(2,1)S(1)} %get-tuple-element.65), channel_id=1, source_target_pairs={{0,1},{1,0},{2,3},{3,2},{4,5},{5,4},{6,7},{7,6},{8,9},{9,8},{10,11... | collective-permute-start | bytes 700424 | tf_op jit(solution)/shard_map/ppermute | solution.py:34
  14.5 0.3 collective-permute-start.5
  14.8 1.8 %collective-permute-start.6 = (bf16[656,128]{1,0:T(8,128)(2,1)S(1)}, bf16[656,128]{1,0:T(8,128)(2,1)S(1)}, u32[]{:S(2)}, u32[]{:S(2)}) collective-permute-start(bf16[656,128]{1,0:T(8,128)(2,1)S(1)} %get-tuple-element.74), channel_id=1, source_target_pairs={{0,3},{1,2},{2,1},{3,0},{4,7},{5,6},{6,5},{7,4},{8,11},{9,10},{10,... | collective-permute-start | bytes 503816 | tf_op jit(solution)/shard_map/ppermute | solution.py:34
  16.6 1.0 %gates.1 = bf16[4,128,1024]{2,1,0:T(8,128)(2,1)} custom-call(bf16[128,4096]{1,0:T(8,128)(2,1)S(1)} %copy-done), custom_call_target="tpu_custom_call" | custom-call | flops 1 | bytes 1 | tf_op jit(solution)/shard_map/gates/pallas_call | solution.py:318
  17.7 0.3 collective-permute-start.2
  18.0 0.7 %copy-done.1 = bf16[912,128]{1,0:T(8,128)(2,1)} copy-done((bf16[912,128]{1,0:T(8,128)(2,1)}, bf16[912,128]{1,0:T(8,128)(2,1)S(1)}, u32[]{:S(2)}) %copy-start.1) | copy-done | bytes 233496
  18.7 1.0 %collective-permute-start.3 = (bf16[912,128]{1,0:T(8,128)(2,1)}, bf16[912,128]{1,0:T(8,128)(2,1)}, u32[]{:S(2)}, u32[]{:S(2)}) collective-permute-start(bf16[912,128]{1,0:T(8,128)(2,1)} %get-tuple-element.70), channel_id=1, source_target_pairs={{0,3},{1,2},{2,1},{3,0},{4,7},{5,6},{6,5},{7,4},{8,11},{9,10},{10,... | collective-permute-start | bytes 700424 | tf_op jit(solution)/shard_map/ppermute | solution.py:34
  19.7 4.7 %all-to-all-start = ((bf16[4,128,1024]{2,1,0:T(8,128)(2,1)}), bf16[4,128,1024]{2,1,0:T(8,128)(2,1)}, u32[]{:S(2)}, u32[]{:S(2)}) async-start(bf16[4,128,1024]{2,1,0:T(8,128)(2,1)} %gates.1), calls=%async_computation | async-start | bytes 2097152 | tf_op jit(solution)/shard_map/all_to_all | solution.py:445
  24.4 0.6 %collective-permute-done.6.rest_3_ = bf16[656,128]{1,0:T(8,128)(2,1)S(1)} collective-permute-done((bf16[656,128]{1,0:T(8,128)(2,1)S(1)}, bf16[656,128]{1,0:T(8,128)(2,1)S(1)}, u32[]{:S(2)}, u32[]{:S(2)}) %collective-permute-start.6) | collective-permute-done | bytes 167968 | tf_op jit(solution)/shard_map/ppermute | solution.py:34
  25.1 1.4 %state0.1 = (bf16[512,512]{1,0:T(8,128)(2,1)S(1)}, bf16[512,512]{1,0:T(8,128)(2,1)S(1)}, bf16[512,128]{1,0:T(8,128)(2,1)S(1)}, f32[4,8,128]{2,1,0:T(8,128)S(1)},...) custom-call(f32[16]{0:T(128)S(1)} %copy-done.5, f32[16]{0:T(128)S(1)} %copy-done.6, ...), custom_call_target="tpu_custom_call" | custom-call | flops 999999995904 | bytes 1000000000 | tf_op jit(solution)/shard_map/state0/pallas_call | solution.py:318
  26.5 1.3 %collective-permute-start.10 = (bf16[144,512]{1,0:T(8,128)(2,1)S(1)}, bf16[144,512]{1,0:T(8,128)(2,1)S(1)}, u32[]{:S(2)}, u32[]{:S(2)}) collective-permute-start(bf16[144,512]{1,0:T(8,128)(2,1)S(1)} %get-tuple-element.92), channel_id=1, source_target_pairs={{0,4},{4,8},{8,12},{1,5},{5,9},{9,13},{2,6},{6,10},{10,14},{3,7},{... | collective-permute-start | bytes 442376 | tf_op jit(solution)/shard_map/ppermute | solution.py:39
  27.8 1.3 %collective-permute-start.11 = (bf16[144,512]{1,0:T(8,128)(2,1)S(1)}, bf16[144,512]{1,0:T(8,128)(2,1)S(1)}, u32[]{:S(2)}, u32[]{:S(2)}) collective-permute-start(bf16[144,512]{1,0:T(8,128)(2,1)S(1)} %get-tuple-element.92), channel_id=1, source_target_pairs={{0,8},{4,12},{1,9},{5,13},{2,10},{6,14},{3,11},{7,15},{16,24},{20,... | collective-permute-start | bytes 442376 | tf_op jit(solution)/shard_map/ppermute | solution.py:39
  29.1 1.3 %collective-permute-start.12 = (bf16[144,512]{1,0:T(8,128)(2,1)S(1)}, bf16[144,512]{1,0:T(8,128)(2,1)S(1)}, u32[]{:S(2)}, u32[]{:S(2)}) collective-permute-start(bf16[144,512]{1,0:T(8,128)(2,1)S(1)} %get-tuple-element.92), channel_id=1, source_target_pairs={{0,12},{1,13},{2,14},{3,15},{16,28},{17,29},{18,30},{19,31}} | collective-permute-start | bytes 442376 | tf_op jit(solution)/shard_map/ppermute | solution.py:39
  30.4 5.1 %collective-permute-done.3.rest_3_ = bf16[912,128]{1,0:T(8,128)(2,1)} collective-permute-done((bf16[912,128]{1,0:T(8,128)(2,1)}, bf16[912,128]{1,0:T(8,128)(2,1)}, u32[]{:S(2)}, u32[]{:S(2)}) %collective-permute-start.3) | collective-permute-done | bytes 233504 | tf_op jit(solution)/shard_map/ppermute | solution.py:34
  35.5 2.5 %state1.1 = (bf16[512,512]{1,0:T(8,128)(2,1)S(1)}, bf16[512,512]{1,0:T(8,128)(2,1)S(1)}, bf16[512,128]{1,0:T(8,128)(2,1)S(1)}, f32[4,8,128]{2,1,0:T(8,128)S(1)},...) custom-call(f32[16]{0:T(128)S(1)} %copy-done.5, f32[16]{0:T(128)S(1)} %copy-done.6, ...), custom_call_target="tpu_custom_call" | custom-call | flops 1 | bytes 1 | tf_op jit(solution)/shard_map/state1/pallas_call | solution.py:318
  38.0 1.3 %collective-permute-start.7 = (bf16[144,512]{1,0:T(8,128)(2,1)}, bf16[144,512]{1,0:T(8,128)(2,1)}, u32[]{:S(2)}, u32[]{:S(2)}) collective-permute-start(bf16[144,512]{1,0:T(8,128)(2,1)} %get-tuple-element.87), channel_id=1, source_target_pairs={{0,4},{4,8},{8,12},{1,5},{5,9},{9,13},{2,6},{6,10},{10,14},{3,7},{... | collective-permute-start | bytes 442376 | tf_op jit(solution)/shard_map/ppermute | solution.py:39
  39.3 1.3 %collective-permute-start.8 = (bf16[144,512]{1,0:T(8,128)(2,1)}, bf16[144,512]{1,0:T(8,128)(2,1)}, u32[]{:S(2)}, u32[]{:S(2)}) collective-permute-start(bf16[144,512]{1,0:T(8,128)(2,1)} %get-tuple-element.87), channel_id=1, source_target_pairs={{0,8},{4,12},{1,9},{5,13},{2,10},{6,14},{3,11},{7,15},{16,24},{20,... | collective-permute-start | bytes 442376 | tf_op jit(solution)/shard_map/ppermute | solution.py:39
  40.6 0.0 copy-start.7
  40.6 0.6 %copy-done.7 = f32[16]{0:T(128)S(1)} copy-done((f32[16]{0:T(128)S(1)}, f32[16]{0:T(128)}, u32[]{:S(2)}) %copy-start.7) | copy-done | bytes 88
  41.3 2.5 %mix.1 = (bf16[512,128]{1,0:T(8,128)(2,1)S(1)}, f32[512,512]{1,0:T(8,128)S(1)}, bf16[512,128]{1,0:T(8,128)(2,1)S(1)}, f32[512,512]{1,0:T(8,128)S(1)}) custom-call(f32[16]{0:T(128)S(1)} %copy-done.7, bf16[912,128]{1,0:T(8,128)(2,1)S(1)} %get-tuple-element.67.rest_0_, bf16[912,128]{1,0:T(8,128)(2,1)S(1)} %copy-done.2, ...), custom_call_target="tpu_custom_call" | custom-call | flops 1 | bytes 1 | tf_op jit(solution)/shard_map/mix/pallas_call | solution.py:318
  43.8 0.0 copy-start.8
  43.8 1.3 %collective-permute-start.9 = (bf16[144,512]{1,0:T(8,128)(2,1)}, bf16[144,512]{1,0:T(8,128)(2,1)}, u32[]{:S(2)}, u32[]{:S(2)}) collective-permute-start(bf16[144,512]{1,0:T(8,128)(2,1)} %get-tuple-element.87), channel_id=1, source_target_pairs={{0,12},{1,13},{2,14},{3,15},{16,28},{17,29},{18,30},{19,31}} | collective-permute-start | bytes 442376 | tf_op jit(solution)/shard_map/ppermute | solution.py:39
  45.2 3.0 %out0.1.rest_5_ = bf16[512,1024]{1,0:T(8,128)(2,1)} custom-call(f32[1,1024]{1,0:T(1,128)S(1)} %bitcast.3, bf16[4,128,1024]{2,1,0:T(8,128)(2,1)} %all-to-all-done.gate_ref, bf16[512,128]{1,0:T(8,128)(2,1)S(1)} %get-tuple-element.88.c_ref, f32[512,512]{1,0:T(8,128)S(1)} %get-tuple-element.89.mixed_ref, f32[4,8,128]{2,1,0:T(8,128)S(1)} %get-tuple-element.78.rest_7_.grow_ref, ...), custom_call_target="tpu_custom_call" | custom-call | flops 999999995904 | bytes 1000000000 | tf_op jit(solution)/shard_map/out0/pallas_call | solution.py:472
  48.1 8.1 %collective-permute-done.8.rest_3_ = bf16[144,512]{1,0:T(8,128)(2,1)} collective-permute-done((bf16[144,512]{1,0:T(8,128)(2,1)}, bf16[144,512]{1,0:T(8,128)(2,1)}, u32[]{:S(2)}, u32[]{:S(2)}) %collective-permute-start.8) | collective-permute-done | bytes 147488 | tf_op jit(solution)/shard_map/ppermute | solution.py:39
  56.2 3.1 %out1.1 = bf16[512,1024]{1,0:T(8,128)(2,1)} custom-call(f32[1,1024]{1,0:T(1,128)S(1)} %bitcast.4, bf16[4,128,1024]{2,1,0:T(8,128)(2,1)} %all-to-all-done.gate_ref, bf16[512,128]{1,0:T(8,128)(2,1)S(1)} %get-tuple-element.83.c_ref, f32[512,512]{1,0:T(8,128)S(1)} %get-tuple-element.84.mixed_ref, ...), custom_call_target="tpu_custom_call", output_to_operand_aliasing={{}: (10, {})} | custom-call | flops 999999995904 | bytes 1000000000 | tf_op jit(solution)/shard_map/out1/pallas_call | solution.py:472
  (24 shorter events, 0.1 us)
Async XLA Ops:
  1.6 5.1 %collective-permute-start = (bf16[4,6144]{1,0:T(4,128)(2,1)}, bf16[4,6144]{1,0:T(4,128)(2,1)}, u32[]{:S(2)}, u32[]{:S(2)}) collective-permute-start(bf16[4,6144]{1,0:T(4,128)(2,1)} %rim.1), channel_id=1, source_target_pairs={{0,1},{1,2},{2,3},{3,4},{4,5},{5,6},{6,7},{7,8},{8,9},{9,10},{10,1... | collective-permute-start | bytes 147464 | tf_op jit(solution)/shard_map/ppermute | solution.py:39
  8.7 8.0 %copy-start = (bf16[128,4096]{1,0:T(8,128)(2,1)S(1)}, bf16[128,4096]{1,0:T(8,128)(2,1)}, u32[]{:S(2)}) copy-start(bf16[128,4096]{1,0:T(8,128)(2,1)} %z_ref.1) | copy-start | bytes 3145732
  12.3 5.6 %collective-permute-start.1 = (bf16[912,128]{1,0:T(8,128)(2,1)S(1)}, bf16[912,128]{1,0:T(8,128)(2,1)S(1)}, u32[]{:S(2)}, u32[]{:S(2)}) collective-permute-start(bf16[912,128]{1,0:T(8,128)(2,1)S(1)} %get-tuple-element.65), channel_id=1, source_target_pairs={{0,1},{1,0},{2,3},{3,2},{4,5},{5,4},{6,7},{7,6},{8,9},{9,8},{10,11... | collective-permute-start | bytes 700424 | tf_op jit(solution)/shard_map/ppermute | solution.py:34
  14.5 10.0 %collective-permute-start.4 = (bf16[656,128]{1,0:T(8,128)(2,1)S(1)}, bf16[656,128]{1,0:T(8,128)(2,1)S(1)}, u32[]{:S(2)}, u32[]{:S(2)}) collective-permute-start(bf16[656,128]{1,0:T(8,128)(2,1)S(1)} %get-tuple-element.72), channel_id=1, source_target_pairs={{0,1},{1,0},{2,3},{3,2},{4,5},{5,4},{6,7},{7,6},{8,9},{9,8},{10,11... | collective-permute-start | bytes 503816 | tf_op jit(solution)/shard_map/ppermute | solution.py:34
  14.5 10.0 %collective-permute-start.5 = (bf16[656,128]{1,0:T(8,128)(2,1)S(1)}, bf16[656,128]{1,0:T(8,128)(2,1)S(1)}, u32[]{:S(2)}, u32[]{:S(2)}) collective-permute-start(bf16[656,128]{1,0:T(8,128)(2,1)S(1)} %get-tuple-element.73), channel_id=1, source_target_pairs={{0,2},{1,3},{2,0},{3,1},{4,6},{5,7},{6,4},{7,5},{8,10},{9,11},{10,... | collective-permute-start | bytes 503816 | tf_op jit(solution)/shard_map/ppermute | solution.py:34
  14.8 10.3 %collective-permute-start.6 = (bf16[656,128]{1,0:T(8,128)(2,1)S(1)}, bf16[656,128]{1,0:T(8,128)(2,1)S(1)}, u32[]{:S(2)}, u32[]{:S(2)}) collective-permute-start(bf16[656,128]{1,0:T(8,128)(2,1)S(1)} %get-tuple-element.74), channel_id=1, source_target_pairs={{0,3},{1,2},{2,1},{3,0},{4,7},{5,6},{6,5},{7,4},{8,11},{9,10},{10,... | collective-permute-start | bytes 503816 | tf_op jit(solution)/shard_map/ppermute | solution.py:34
  17.7 7.4 %copy-start.5 = (f32[16]{0:T(128)S(1)}, f32[16]{0:T(128)}, u32[]{:S(2)}) copy-start(f32[16]{0:T(128)} %bias_ref.3) | copy-start | bytes 196
  17.7 7.4 %copy-start.6 = (f32[16]{0:T(128)S(1)}, f32[16]{0:T(128)}, u32[]{:S(2)}) copy-start(f32[16]{0:T(128)} %log_ref.3) | copy-start | bytes 196
  17.7 12.7 %collective-permute-start.2 = (bf16[912,128]{1,0:T(8,128)(2,1)}, bf16[912,128]{1,0:T(8,128)(2,1)}, u32[]{:S(2)}, u32[]{:S(2)}) collective-permute-start(bf16[912,128]{1,0:T(8,128)(2,1)} %get-tuple-element.69), channel_id=1, source_target_pairs={{0,2},{1,3},{2,0},{3,1},{4,6},{5,7},{6,4},{7,5},{8,10},{9,11},{10,... | collective-permute-start | bytes 700424 | tf_op jit(solution)/shard_map/ppermute | solution.py:34
  18.0 0.7 %copy-start.1 = (bf16[912,128]{1,0:T(8,128)(2,1)}, bf16[912,128]{1,0:T(8,128)(2,1)S(1)}, u32[]{:S(2)}) copy-start(bf16[912,128]{1,0:T(8,128)(2,1)S(1)} %collective-permute-done.1.rest_1_) | copy-start | bytes 700420
  18.7 16.8 %collective-permute-start.3 = (bf16[912,128]{1,0:T(8,128)(2,1)}, bf16[912,128]{1,0:T(8,128)(2,1)}, u32[]{:S(2)}, u32[]{:S(2)}) collective-permute-start(bf16[912,128]{1,0:T(8,128)(2,1)} %get-tuple-element.70), channel_id=1, source_target_pairs={{0,3},{1,2},{2,1},{3,0},{4,7},{5,6},{6,5},{7,4},{8,11},{9,10},{10,... | collective-permute-start | bytes 700424 | tf_op jit(solution)/shard_map/ppermute | solution.py:34
  19.7 25.4 %all-to-all-start = ((bf16[4,128,1024]{2,1,0:T(8,128)(2,1)}), bf16[4,128,1024]{2,1,0:T(8,128)(2,1)}, u32[]{:S(2)}, u32[]{:S(2)}) async-start(bf16[4,128,1024]{2,1,0:T(8,128)(2,1)} %gates.1), calls=%async_computation | async-start | bytes 2097152 | tf_op jit(solution)/shard_map/all_to_all | solution.py:445
  25.1 10.4 %copy-start.2 = (bf16[912,128]{1,0:T(8,128)(2,1)S(1)}, bf16[912,128]{1,0:T(8,128)(2,1)}, u32[]{:S(2)}) copy-start(bf16[912,128]{1,0:T(8,128)(2,1)} %copy-done.1) | copy-start | bytes 700420
  26.5 17.3 %collective-permute-start.10 = (bf16[144,512]{1,0:T(8,128)(2,1)S(1)}, bf16[144,512]{1,0:T(8,128)(2,1)S(1)}, u32[]{:S(2)}, u32[]{:S(2)}) collective-permute-start(bf16[144,512]{1,0:T(8,128)(2,1)S(1)} %get-tuple-element.92), channel_id=1, source_target_pairs={{0,4},{4,8},{8,12},{1,5},{5,9},{9,13},{2,6},{6,10},{10,14},{3,7},{... | collective-permute-start | bytes 442376 | tf_op jit(solution)/shard_map/ppermute | solution.py:39
  27.8 17.3 %collective-permute-start.11 = (bf16[144,512]{1,0:T(8,128)(2,1)S(1)}, bf16[144,512]{1,0:T(8,128)(2,1)S(1)}, u32[]{:S(2)}, u32[]{:S(2)}) collective-permute-start(bf16[144,512]{1,0:T(8,128)(2,1)S(1)} %get-tuple-element.92), channel_id=1, source_target_pairs={{0,8},{4,12},{1,9},{5,13},{2,10},{6,14},{3,11},{7,15},{16,24},{20,... | collective-permute-start | bytes 442376 | tf_op jit(solution)/shard_map/ppermute | solution.py:39
  29.1 16.1 %collective-permute-start.12 = (bf16[144,512]{1,0:T(8,128)(2,1)S(1)}, bf16[144,512]{1,0:T(8,128)(2,1)S(1)}, u32[]{:S(2)}, u32[]{:S(2)}) collective-permute-start(bf16[144,512]{1,0:T(8,128)(2,1)S(1)} %get-tuple-element.92), channel_id=1, source_target_pairs={{0,12},{1,13},{2,14},{3,15},{16,28},{17,29},{18,30},{19,31}} | collective-permute-start | bytes 442376 | tf_op jit(solution)/shard_map/ppermute | solution.py:39
  38.0 5.8 %copy-start.3 = (f32[4,8,128]{2,1,0:T(8,128)}, f32[4,8,128]{2,1,0:T(8,128)S(1)}, u32[]{:S(2)}) copy-start(f32[4,8,128]{2,1,0:T(8,128)S(1)} %get-tuple-element.82.rest_11_.grow_ref) | copy-start | bytes 49156
  38.0 10.1 %collective-permute-start.7 = (bf16[144,512]{1,0:T(8,128)(2,1)}, bf16[144,512]{1,0:T(8,128)(2,1)}, u32[]{:S(2)}, u32[]{:S(2)}) collective-permute-start(bf16[144,512]{1,0:T(8,128)(2,1)} %get-tuple-element.87), channel_id=1, source_target_pairs={{0,4},{4,8},{8,12},{1,5},{5,9},{9,13},{2,6},{6,10},{10,14},{3,7},{... | collective-permute-start | bytes 442376 | tf_op jit(solution)/shard_map/ppermute | solution.py:39
  39.3 16.9 %collective-permute-start.8 = (bf16[144,512]{1,0:T(8,128)(2,1)}, bf16[144,512]{1,0:T(8,128)(2,1)}, u32[]{:S(2)}, u32[]{:S(2)}) collective-permute-start(bf16[144,512]{1,0:T(8,128)(2,1)} %get-tuple-element.87), channel_id=1, source_target_pairs={{0,8},{4,12},{1,9},{5,13},{2,10},{6,14},{3,11},{7,15},{16,24},{20,... | collective-permute-start | bytes 442376 | tf_op jit(solution)/shard_map/ppermute | solution.py:39
  40.6 0.7 %copy-start.7 = (f32[16]{0:T(128)S(1)}, f32[16]{0:T(128)}, u32[]{:S(2)}) copy-start(f32[16]{0:T(128)} %skip_ref.1) | copy-start | bytes 196
  43.8 1.4 %copy-start.8 = (f32[1024]{0:T(1024)S(1)}, f32[1024]{0:T(1024)}, u32[]{:S(2)}) copy-start(f32[1024]{0:T(1024)} %param.23) | copy-start | bytes 12292
  43.8 12.4 %collective-permute-start.9 = (bf16[144,512]{1,0:T(8,128)(2,1)}, bf16[144,512]{1,0:T(8,128)(2,1)}, u32[]{:S(2)}, u32[]{:S(2)}) collective-permute-start(bf16[144,512]{1,0:T(8,128)(2,1)} %get-tuple-element.87), channel_id=1, source_target_pairs={{0,12},{1,13},{2,14},{3,15},{16,28},{17,29},{18,30},{19,31}} | collective-permute-start | bytes 442376 | tf_op jit(solution)/shard_map/ppermute | solution.py:39
  45.1 11.1 %copy-start.4 = (f32[4,8,128]{2,1,0:T(8,128)S(1)}, f32[4,8,128]{2,1,0:T(8,128)}, u32[]{:S(2)}) copy-start(f32[4,8,128]{2,1,0:T(8,128)} %copy-done.3) | copy-start | bytes 49156

commit v3 on v2

--- a/solution.py
+++ b/solution.py
@@ -20,8 +20,9 @@
 RIM = 4
 EXTRA = 16
 SHORT = pl.CostEstimate(flops=1, bytes_accessed=1, transcendentals=1)
-LONG = pl.CostEstimate(flops=10**12, bytes_accessed=10**9, transcendentals=1)
+LONG = pl.CostEstimate(flops=10**12, bytes_accessed=1, transcendentals=1)
 ROOM = 12 * 2**20
+COSTS = {"gates": SHORT, "state0": LONG, "state1": LONG, "mix": LONG}
 F32 = jnp.float32
 BF16 = jnp.bfloat16
 
@@ -57,6 +58,12 @@
 def spread(value, columns):
     return lax.dot_general(
         in_three(value), columns, (((0,), (0,)), ((), ())), preferred_element_type=F32
+    )
+
+
+def spread_rows(value, columns):
+    return lax.dot_general(
+        columns, in_three(value), (((0,), (0,)), ((), ())), preferred_element_type=F32
     )
 
 
@@ -205,30 +212,27 @@
             scaled_ref[at, :] = (conv_ref[at, :].astype(F32) * scale).astype(BF16)
         at = slice(span * per_span * rows, (span + 1) * per_span * rows)
         summed = lax.dot_general(
-            b_ref[at, :], scaled_ref[at, :], (((0,), (0,)), ((), ())), preferred_element_type=F32
+            scaled_ref[at, :], b_ref[at, :], (((0,), (0,)), ((), ())), preferred_element_type=F32
         )
-        summed = summed * spread(jnp.exp(running - middle), columns)
+        summed = summed * spread_rows(jnp.exp(running - middle), columns)
         mid_ref[span] = middle
         prior_ref[span] = prior
         if spans > 1:
             ahead_ref[span] = total if total is not None else jnp.zeros_like(summed)
-        total = summed if total is None else total * spread(jnp.exp(running), columns) + summed
+        total = summed if total is None else total * spread_rows(jnp.exp(running), columns) + summed
         prior = prior + running
-    ship_ref[:STATE_DIM, :] = total.astype(BF16)
-    decay = spread(jnp.exp(prior), columns)[:EXTRA]
+    ship_ref[:GROUP_WIDTH, :] = total.astype(BF16)
+    decay = jnp.exp(prior)
     high = decay.astype(BF16).astype(F32)
-    middle = (decay - high).astype(BF16).astype(F32)
-    at = lax.broadcasted_iota(jnp.int32, (EXTRA, GROUP_WIDTH), 0)
-    stacked = jnp.where(at == 0, high, jnp.where(at == 1, middle, decay - high - middle))
-    ship_ref[STATE_DIM:, :] = jnp.where(at < 3, stacked, 0.0).astype(BF16)
+    ship_ref[GROUP_WIDTH:, :] = jnp.concatenate([high, decay - high], axis=0).astype(BF16)
 
 
 def shipped(ref):
-    rows = ref[STATE_DIM:, :].astype(F32)
-    return ref[:STATE_DIM, :].astype(F32), rows[0:1] + rows[1:2] + rows[2:3]
-
-
-def mix_kernel(gd, spans, tp, skip_ref, *rest):
+    rows = ref[GROUP_WIDTH:, :].astype(F32)
+    return ref[:GROUP_WIDTH, :].astype(F32), rows[:PER_GROUP] + rows[PER_GROUP:]
+
+
+def mix_kernel(gd, spans, tp, skip_ref, gate_ref, *rest):
     pieces, rest = rest[:tp], rest[tp:]
     held, outs = rest[: 4 * gd], rest[4 * gd :]
     rows = outs[0].shape[0] // tp
@@ -238,7 +242,7 @@
     columns = head_columns()
     for group in range(gd):
         conv_ref, scaled_ref, b_ref, grow_ref = held[4 * group : 4 * group + 4]
-        c_ref, mixed_ref = outs[2 * group : 2 * group + 2]
+        c_ref, plain_ref, slope_ref = outs[3 * group : 3 * group + 3]
         first = (X_TILES + 1 + group) * rows + EXTRA
         for slot in range(tp):
             at = pl.ds(pl.multiple_of(partner(me, slot) * rows, rows), rows)
@@ -256,12 +260,19 @@
             s_at = lax.broadcasted_iota(jnp.int32, scores.shape, 1) - (at.start - inside.start)
             masked = jnp.where(s_at <= t_at, scores, 0.0).astype(BF16)
             mixed = jnp.dot(masked, scaled_ref[inside, :], preferred_element_type=F32)
-            grow = [spread(grow_ref[other], columns) for other in range(place, place + join)]
-            mixed = mixed * jnp.concatenate(grow, axis=0)
-            mixed_ref[at, :] = mixed + skip * conv_ref[at, :].astype(F32)
-
-
-def out_kernel(group, spans, states, gain_ref, gate_ref, c_ref, mixed_ref, grow_ref, *rest):
+            grow = jnp.concatenate(
+                [spread(grow_ref[other], columns) for other in range(place, place + join)], axis=0
+            )
+            mixed = mixed * grow + skip * conv_ref[at, :].astype(F32)
+            z_at = group * GROUP_WIDTH
+            gate = gate_ref[place : place + join, :, z_at : z_at + GROUP_WIDTH]
+            gate = gate.reshape(join * rows, GROUP_WIDTH).astype(F32)
+            gate = gate / (1.0 + jnp.exp(-gate))
+            plain_ref[at, :] = mixed * gate
+            slope_ref[at, :] = grow * gate
+
+
+def out_kernel(spans, states, gain_ref, c_ref, plain_ref, slope_ref, *rest):
     mid_ref, prior_ref = rest[:2]
     rest = rest[2:]
     ahead_ref = None
@@ -269,29 +280,26 @@
         ahead_ref, rest = rest[0], rest[1:]
     sent, rest = rest[:states], rest[states:]
     out_ref = rest[-1]
-    tp, rows, _ = gate_ref.shape
-    per_span = tp // spans
     columns = head_columns()
+    ctx = lax.axis_index("ctx")
     state = None
-    for ref in reversed(sent):
-        value, decay = shipped(ref)
-        state = value if state is None else state * decay + value
-    join = 2 if per_span % 2 == 0 else 1
+    for steps in range(states, 0, -1):
+        value, decay = shipped(sent[steps - 1])
+        value = jnp.where(ctx >= steps, value, 0.0)
+        state = value if state is None else state * spread_rows(decay, columns) + value
+    span_rows = c_ref.shape[0] // spans
+    tall = min(span_rows, 256)
     for span in range(spans):
         start = state
         if spans > 1:
-            start = start * spread(jnp.exp(prior_ref[span]), columns) + ahead_ref[span]
-        start = (start * spread(jnp.exp(mid_ref[span]), columns)).astype(BF16)
-        for first in range(span * per_span, (span + 1) * per_span, join):
-            tall = join * rows
-            at = slice(first * rows, first * rows + tall)
-            carried = jnp.dot(c_ref[at, :], start, preferred_element_type=F32)
-            grow = [spread(grow_ref[place], columns) for place in range(first, first + join)]
-            mixed = mixed_ref[at, :] + carried * jnp.concatenate(grow, axis=0)
-            z_at = group * GROUP_WIDTH
-            gate = gate_ref[first : first + join, :, z_at : z_at + GROUP_WIDTH]
-            gate = gate.reshape(tall, GROUP_WIDTH).astype(F32)
-            gated = mixed * (gate / (1.0 + jnp.exp(-gate)))
+            start = start * spread_rows(jnp.exp(prior_ref[span]), columns) + ahead_ref[span]
+        start = (start * spread_rows(jnp.exp(mid_ref[span]), columns)).astype(BF16)
+        for first in range(span * span_rows, (span + 1) * span_rows, tall):
+            at = slice(first, first + tall)
+            carried = lax.dot_general(
+                c_ref[at, :], start, (((1,), (1,)), ((), ())), preferred_element_type=F32
+            )
+            gated = plain_ref[at, :] + carried * slope_ref[at, :]
             square = jnp.mean(gated * gated, axis=-1, keepdims=True)
             out_ref[at, :] = (gated * lax.rsqrt(square + 1e-5) * gain_ref[...]).astype(BF16)
 
@@ -312,7 +320,7 @@
     return [pl.BlockSpec(memory_space=pltpu.SMEM)] * count
 
 
-def call(kernel, ins, outs, scratch, scalars=0, near=(), cost=LONG, name=None):
+def call(kernel, ins, outs, scratch, scalars=0, near=(), name=None):
     ins = [close(value) if place in near else value for place, value in enumerate(ins)]
     outs = [pltpu.VMEM(out.shape, out.dtype) for out in outs]
     return pl.pallas_call(
@@ -322,32 +330,35 @@
         out_shape=outs,
         scratch_shapes=scratch,
         compiler_params=pltpu.CompilerParams(vmem_limit_bytes=ROOM),
-        cost_estimate=cost,
+        cost_estimate=COSTS.get(name, LONG),
         name=name,
     )(*ins)
+
+
+def joined(ship):
+    rows = ship[GROUP_WIDTH:].astype(F32)
+    return rows[:PER_GROUP] + rows[PER_GROUP:]
+
+
+def packed(state, decay):
+    high = decay.astype(BF16).astype(F32)
+    return jnp.concatenate([state, high, decay - high], axis=0).astype(BF16)
 
 
 def scanned(ship):
     count = lax.axis_size("ctx")
     if count <= 4:
-        return [from_behind(ship, "ctx", steps) for steps in range(1, count)]
-    state = ship[:STATE_DIM].astype(F32)
-    decay = jnp.sum(ship[STATE_DIM : STATE_DIM + 3].astype(F32), axis=0, keepdims=True)
-
-    def packed(state, decay):
-        high = decay.astype(BF16).astype(F32)
-        middle = (decay - high).astype(BF16).astype(F32)
-        rows = [state, high, middle, decay - high - middle]
-        rows.append(jnp.zeros((EXTRA - 3, GROUP_WIDTH), F32))
-        return jnp.concatenate(rows, axis=0).astype(BF16)
-
+        return [
+            lax.ppermute(ship, "ctx", [(i, (i + steps) % count) for i in range(count)])
+            for steps in range(1, count)
+        ]
+    state, decay = ship[:GROUP_WIDTH].astype(F32), joined(ship)
     steps = 1
     while steps < count:
         other = from_behind(packed(state, decay), "ctx", steps)
-        state = other[:STATE_DIM].astype(F32) * decay + state
-        decay = decay * jnp.sum(
-            other[STATE_DIM : STATE_DIM + 3].astype(F32), axis=0, keepdims=True
-        )
+        scale = jnp.repeat(decay, HEAD_DIM, axis=0)
+        state = other[:GROUP_WIDTH].astype(F32) * scale + state
+        decay = decay * joined(other)
         steps *= 2
     return [from_behind(packed(state, decay), "ctx", 1)]
 
@@ -399,9 +410,6 @@
         name="load",
     )(*used)
     conv_scratch = pltpu.VMEM((8 + rows, LANES), F32)
-    gates = call(
-        gate_kernel, [z_input], [shape((tp, rows, width), BF16)], [], cost=SHORT, name="gates"
-    )[0]
     traded = []
     for group in range(gd):
         tall = (X_TILES + 1 + (gd if group == gd - 1 else 0)) * rows + EXTRA
@@ -413,9 +421,13 @@
             near=range(8),
             name=f"send{group}",
         )
-        rim, parts = lax.optimization_barrier((rim, parts))
+        rim, parts, z_input = lax.optimization_barrier((rim, parts, z_input))
         traded.append(trade(parts))
-    gates, traded[-1][1] = lax.optimization_barrier((gates, traded[-1][1]))
+        if group == 0:
+            gates = call(
+                gate_kernel, [z_input], [shape((tp, rows, width), BF16)], [], name="gates"
+            )[0]
+    gates, traded[0][tp // 2] = lax.optimization_barrier((gates, traded[0][tp // 2]))
     held = []
     for group in range(gd):
         outs = [
@@ -425,42 +437,43 @@
             shape((tp, PER_GROUP, rows), F32),
             shape((spans, PER_GROUP, rows), F32),
             shape((spans, PER_GROUP, rows), F32),
-            shape((STATE_DIM + EXTRA, GROUP_WIDTH), BF16),
+            shape((GROUP_WIDTH + 2 * PER_GROUP, STATE_DIM), BF16),
         ]
         if spans > 1:
-            outs.append(shape((spans, STATE_DIM, GROUP_WIDTH), F32))
+            outs.append(shape((spans, GROUP_WIDTH, STATE_DIM), F32))
         made = call(
             functools.partial(state_kernel, group, tp, spans),
-            [dt_bias, a_log] + traded[group],
+            [far(dt_bias), far(a_log)] + traded[group],
             outs,
             [pltpu.VMEM((tp, PER_GROUP, rows), F32)],
             scalars=2,
             near=range(2, 2 + tp),
-            cost=LONG if group == 0 else SHORT,
             name=f"state{group}",
         )
         ship = made[6]
         kept_values = list(made[:6]) + list(made[7:])
         held.append((kept_values, scanned(ship)))
     gates = lax.all_to_all(gates, "tp", split_axis=0, concat_axis=0, tiled=True)
-    gain = norm_gain.reshape(1, -1)
-    ins = [d_skip] + traded[-1]
+    if gd > 1:
+        first = held[0][1]
+        gates, first[0] = lax.optimization_barrier((gates, first[0]))
+    gain = far(norm_gain.reshape(1, -1))
+    ins = [far(d_skip), gates] + traded[-1]
     for values, _ in held:
         ins += values[:4]
     mixed = call(
         functools.partial(mix_kernel, gd, spans, tp),
         ins,
-        [shape((ctx_rows, STATE_DIM), BF16), shape((ctx_rows, GROUP_WIDTH), F32)] * gd,
+        ([shape((ctx_rows, STATE_DIM), BF16)] + [shape((ctx_rows, GROUP_WIDTH), F32)] * 2) * gd,
         [],
         scalars=1,
         near=range(1, len(ins)),
-        cost=SHORT,
         name="mix",
     )
     out = None
     for group in range(gd):
         values, sent = held[group]
-        ins = [gates, mixed[2 * group], mixed[2 * group + 1]] + values[3:] + sent
+        ins = list(mixed[3 * group : 3 * group + 3]) + values[4:] + sent
         ins = [gain] + [close(value) for value in ins]
         aliases = {}
         specs = [pl.BlockSpec((1, GROUP_WIDTH), lambda i, g=group: (0, g))]
@@ -470,7 +483,7 @@
             ins.append(out)
             specs.append(pl.BlockSpec(memory_space=pl.ANY))
         out = pl.pallas_call(
-            functools.partial(out_kernel, group, spans, len(sent)),
+            functools.partial(out_kernel, spans, len(sent)),
             grid=(1,),
             in_specs=specs,
             out_specs=pl.BlockSpec((ctx_rows, GROUP_WIDTH), lambda i, g=group: (0, g)),

time: 59.9 us -> 55.7 us (0.930)
  the two profiles are of different devices: /device:TPU:25 before, /device:TPU:0 now
where the time goes in v3:
time: 55.7 us; the launch traced here: 55.3 us
  Pallas kernels  24.4 us (44%)
  starting transfers between devices  23.6 us (42%)
  waiting for transfers between devices  7.14 us (13%)
    pallas_call x6, Pallas kernels, call(): pl.pallas_call(kernel, in_specs=smem(scalars) + vmem(len(ins) - scalars),...  16.3 us
    ppermute x6, starting transfers between devices, scanned(): lax.ppermute(ship, 'ctx', [(i, (i + steps) % count) for i in range(count)])  9.89 us
    all_to_all x1, waiting for transfers between devices, shards(): gates = lax.all_to_all(gates, 'tp', split_axis=0, concat_axis=0, tiled=True)  7.11 us
    ppermute x6, starting transfers between devices, swap(): lax.ppermute(value, 'tp', [(i, i ^ slot) for i in range(lax.axis_size('tp...  6.51 us
    pallas_call x2, Pallas kernels, shards(): pl.pallas_call(functools.partial(out_kernel, spans, len(sent)), grid=(1,)...  5.08 us
    all_to_all x1, starting transfers between devices, shards(): gates = lax.all_to_all(gates, 'tp', split_axis=0, concat_axis=0, tiled=True)  4.24 us
    ppermute x1, starting transfers between devices, from_behind(): lax.ppermute(value, axis, [(i, i + steps) for i in range(count - steps)])  3 us
    pallas_call x1, Pallas kernels, shards(): pl.pallas_call(rim_kernel, grid=(1,), in_specs=[pl.BlockSpec((16, x_input...  1.56 us
  transfers between devices with their start and end apart: 14, of which 1 were waited for; matrix products, arithmetic and copies ran while one was open for 0% of the time, Pallas kernels for 32%

profile of v3, /device:TPU:0, one launch (start us, length us, event | category | flops | bytes accessed | tf_op | source)
XLA Modules:
  0.0 55.3 jit_solution(6493174614743102433)
XLA Ops:
  0.0 1.6 %rim.1 = bf16[4,6144]{1,0:T(4,128)(2,1)} custom-call(bf16[128,4096]{1,0:T(8,128)(2,1)} %refs_0_.1, bf16[128,2,1024]{2,1,0:T(2,128)(2,1)} %refs_1_.1), custom_call_target="tpu_custom_call" | custom-call | tf_op jit(solution)/shard_map/rim/pallas_call | solution.py:383
  1.6 3.0 %collective-permute-start = (bf16[4,6144]{1,0:T(4,128)(2,1)}, bf16[4,6144]{1,0:T(4,128)(2,1)}, u32[]{:S(2)}, u32[]{:S(2)}) collective-permute-start(bf16[4,6144]{1,0:T(4,128)(2,1)} %rim.1), channel_id=1, source_target_pairs={{0,1},{1,2},{2,3},{3,4},{4,5},{5,6},{6,7},{7,8},{8,9},{9,10},{10,1... | collective-permute-start | bytes 147464 | tf_op jit(solution)/shard_map/ppermute | solution.py:40
  4.6 1.4 %load.1 = (bf16[128,4096]{1,0:T(8,128)(2,1)S(1)}, bf16[128,2,1024]{2,1,0:T(2,128)(2,1)S(1)}, bf16[64,128]{1,0:T(8,128)(2,1)S(1)}, f32[4,4096]{1,0:T(4,128)S(1)},...) custom-call(bf16[128,4096]{1,0:T(8,128)(2,1)} %refs_0_.1, bf16[128,2,1024]{2,1,0:T(2,128)(2,1)} %refs_1_.1, ...), custom_call_target="tpu_custom_call" | custom-call | flops 999999995904 | bytes 1 | tf_op jit(solution)/shard_map/load/pallas_call | solution.py:402
  6.0 0.0 collective-permute-done.rim_ref
  6.0 2.8 %send0.1 = (bf16[656,128]{1,0:T(8,128)(2,1)S(1)}, bf16[656,128]{1,0:T(8,128)(2,1)}, bf16[656,128]{1,0:T(8,128)(2,1)}, bf16[656,128]{1,0:T(8,128)(2,1)}) custom-call(bf16[128,4096]{1,0:T(8,128)(2,1)S(1)} %get-tuple-element.54.x_ref, bf16[128,2,1024]{2,1,0:T(2,128)(2,1)S(1)} %get-tuple-element.55.bc_ref, bf16[64,128]{1,0:T(8,128)(2,1)S(1)} %get-tuple-element.56.dt_ref, ...), custom_call_target="tpu_custom_call" | custom-call | flops 999999995904 | bytes 1 | tf_op jit(solution)/shard_map/send0/pallas_call | solution.py:326
  8.8 4.2 %collective-permute-start.1 = (bf16[656,128]{1,0:T(8,128)(2,1)}, bf16[656,128]{1,0:T(8,128)(2,1)}, u32[]{:S(2)}, u32[]{:S(2)}) collective-permute-start(bf16[656,128]{1,0:T(8,128)(2,1)} %get-tuple-element.66), channel_id=1, source_target_pairs={{0,2},{1,3},{2,0},{3,1},{4,6},{5,7},{6,4},{7,5},{8,10},{9,11},{10,... | collective-permute-start | bytes 503816 | tf_op jit(solution)/shard_map/ppermute | solution.py:35
  13.0 0.1 collective-permute-start.3
  13.1 3.9 %send1.1 = (bf16[912,128]{1,0:T(8,128)(2,1)S(1)}, bf16[912,128]{1,0:T(8,128)(2,1)}, bf16[912,128]{1,0:T(8,128)(2,1)}, bf16[912,128]{1,0:T(8,128)(2,1)}) custom-call(bf16[128,4096]{1,0:T(8,128)(2,1)S(1)} %get-tuple-element.54.x_ref, bf16[128,2,1024]{2,1,0:T(2,128)(2,1)S(1)} %get-tuple-element.55.bc_ref, bf16[64,128]{1,0:T(8,128)(2,1)S(1)} %get-tuple-element.56.dt_ref, ...), custom_call_target="tpu_custom_call" | custom-call | flops 999999995904 | bytes 1 | tf_op jit(solution)/shard_map/send1/pallas_call | solution.py:326
  17.0 1.0 %gates.1 = bf16[4,128,1024]{2,1,0:T(8,128)(2,1)} custom-call(bf16[128,4096]{1,0:T(8,128)(2,1)S(1)} %copy-done), custom_call_target="tpu_custom_call" | custom-call | flops 1 | bytes 1 | tf_op jit(solution)/shard_map/gates/pallas_call | solution.py:326
  18.0 0.4 collective-permute-start.5
  18.5 1.6 %collective-permute-start.6 = (bf16[912,128]{1,0:T(8,128)(2,1)}, bf16[912,128]{1,0:T(8,128)(2,1)}, u32[]{:S(2)}, u32[]{:S(2)}) collective-permute-start(bf16[912,128]{1,0:T(8,128)(2,1)} %get-tuple-element.81), channel_id=1, source_target_pairs={{0,2},{1,3},{2,0},{3,1},{4,6},{5,7},{6,4},{7,5},{8,10},{9,11},{10,... | collective-permute-start | bytes 700424 | tf_op jit(solution)/shard_map/ppermute | solution.py:35
  20.1 0.1 collective-permute-start.7
  20.2 0.0 collective-permute-done.2.rest_1_
  20.2 0.0 collective-permute-done.3.rest_3_
  20.2 2.7 %state0.1 = (bf16[512,512]{1,0:T(8,128)(2,1)S(1)}, bf16[512,512]{1,0:T(8,128)(2,1)S(1)}, bf16[512,128]{1,0:T(8,128)(2,1)S(1)}, f32[4,8,128]{2,1,0:T(8,128)S(1)},...) custom-call(f32[16]{0:T(128)} %bias_ref.3, f32[16]{0:T(128)} %log_ref.3, ...), custom_call_target="tpu_custom_call" | custom-call | flops 999999995904 | bytes 1 | tf_op jit(solution)/shard_map/state0/pallas_call | solution.py:326
  22.9 2.7 %collective-permute-start.4 = (bf16[528,128]{1,0:T(8,128)(2,1)}, bf16[528,128]{1,0:T(8,128)(2,1)}, u32[]{:S(2)}, u32[]{:S(2)}) collective-permute-start(bf16[528,128]{1,0:T(8,128)(2,1)} %get-tuple-element.72), channel_id=1, source_target_pairs={{0,4},{4,8},{8,12},{12,0},{1,5},{5,9},{9,13},{13,1},{2,6},{6,10},{... | collective-permute-start | bytes 405512 | tf_op jit(solution)/shard_map/ppermute | solution.py:352
  25.6 2.6 %collective-permute-start.11 = (bf16[528,128]{1,0:T(8,128)(2,1)}, bf16[528,128]{1,0:T(8,128)(2,1)}, u32[]{:S(2)}, u32[]{:S(2)}) collective-permute-start(bf16[528,128]{1,0:T(8,128)(2,1)} %get-tuple-element.72), channel_id=1, source_target_pairs={{0,8},{4,12},{8,0},{12,4},{1,9},{5,13},{9,1},{13,5},{2,10},{6,14},... | collective-permute-start | bytes 405512 | tf_op jit(solution)/shard_map/ppermute | solution.py:352
  28.2 4.2 %all-to-all-start = ((bf16[4,128,1024]{2,1,0:T(8,128)(2,1)}), bf16[4,128,1024]{2,1,0:T(8,128)(2,1)}, u32[]{:S(2)}, u32[]{:S(2)}) async-start(bf16[4,128,1024]{2,1,0:T(8,128)(2,1)} %gates.1), calls=%async_computation | async-start | bytes 2097152 | tf_op jit(solution)/shard_map/all_to_all | solution.py:456
  32.4 0.0 collective-permute-done.5.rest_1_
  32.4 1.4 %collective-permute-start.12 = (bf16[528,128]{1,0:T(8,128)(2,1)}, bf16[528,128]{1,0:T(8,128)(2,1)}, u32[]{:S(2)}, u32[]{:S(2)}) collective-permute-start(bf16[528,128]{1,0:T(8,128)(2,1)} %get-tuple-element.72), channel_id=1, source_target_pairs={{0,12},{4,0},{8,4},{12,8},{1,13},{5,1},{9,5},{13,9},{2,14},{6,2},{... | collective-permute-start | bytes 405512 | tf_op jit(solution)/shard_map/ppermute | solution.py:352
  33.8 2.8 %state1.1 = (bf16[512,512]{1,0:T(8,128)(2,1)S(1)}, bf16[512,512]{1,0:T(8,128)(2,1)S(1)}, bf16[512,128]{1,0:T(8,128)(2,1)S(1)}, f32[4,8,128]{2,1,0:T(8,128)S(1)},...) custom-call(f32[16]{0:T(128)} %bias_ref.3, f32[16]{0:T(128)} %log_ref.3, ...), custom_call_target="tpu_custom_call" | custom-call | flops 999999995904 | bytes 1 | tf_op jit(solution)/shard_map/state1/pallas_call | solution.py:326
  36.6 2.2 %collective-permute-start.10 = (bf16[528,128]{1,0:T(8,128)(2,1)}, bf16[528,128]{1,0:T(8,128)(2,1)}, u32[]{:S(2)}, u32[]{:S(2)}) collective-permute-start(bf16[528,128]{1,0:T(8,128)(2,1)} %get-tuple-element.96), channel_id=1, source_target_pairs={{0,12},{4,0},{8,4},{12,8},{1,13},{5,1},{9,5},{13,9},{2,14},{6,2},{... | collective-permute-start | bytes 405512 | tf_op jit(solution)/shard_map/ppermute | solution.py:352
  38.8 0.0 collective-permute-start.8
  38.8 1.0 %collective-permute-start.9 = (bf16[528,128]{1,0:T(8,128)(2,1)}, bf16[528,128]{1,0:T(8,128)(2,1)}, u32[]{:S(2)}, u32[]{:S(2)}) collective-permute-start(bf16[528,128]{1,0:T(8,128)(2,1)} %get-tuple-element.96), channel_id=1, source_target_pairs={{0,8},{4,12},{8,0},{12,4},{1,9},{5,13},{9,1},{13,5},{2,10},{6,14},... | collective-permute-start | bytes 405512 | tf_op jit(solution)/shard_map/ppermute | solution.py:352
  39.8 7.1 %all-to-all-done.gate_ref = bf16[4,128,1024]{2,1,0:T(8,128)(2,1)} async-done(((bf16[4,128,1024]{2,1,0:T(8,128)(2,1)}), bf16[4,128,1024]{2,1,0:T(8,128)(2,1)}, u32[]{:S(2)}, u32[]{:S(2)}) %all-to-all-start) | async-done | bytes 1048608 | tf_op jit(solution)/shard_map/all_to_all | solution.py:456
  46.9 3.2 %mix.1 = (bf16[512,128]{1,0:T(8,128)(2,1)S(1)}, f32[512,512]{1,0:T(8,128)S(1)}, f32[512,512]{1,0:T(8,128)S(1)}, bf16[512,128]{1,0:T(8,128)(2,1)S(1)}, f32[512,512]{1,0:T(8,128)S(1)}, /*index=5*/f32[512,512]{1,0:T(8,128)S(1)}) custom-call(f32[16]{0:T(128)} %skip_ref.1, bf16[4,128,1024]{2,1,0:T(8,128)(2,1)} %all-to-all-done.gate_ref, ...), custom_call_target="tpu_custom_call" | custom-call | flops 999999995904 | bytes 1 | tf_op jit(solution)/shard_map/mix/pallas_call | solution.py:326
  50.1 0.0 collective-permute-done.11.rest_3_
  50.2 2.5 %out0.1.rest_5_ = bf16[512,1024]{1,0:T(8,128)(2,1)} custom-call(f32[1,1024]{1,0:T(1,128)} %bitcast.5, bf16[512,128]{1,0:T(8,128)(2,1)S(1)} %get-tuple-element.97.c_ref, f32[512,512]{1,0:T(8,128)S(1)} %get-tuple-element.98.plain_ref, f32[512,512]{1,0:T(8,128)S(1)} %get-tuple-element.99.slope_ref, f32[1,8,128]{2,1,0:T(8,128)S(1)} %get-tuple-element.100.rest_0_, ...), custom_call_target="tpu_custom_call" | custom-call | flops 999999995904 | bytes 1 | tf_op jit(solution)/shard_map/out0/pallas_call | solution.py:485
  52.7 0.0 collective-permute-done.10.rest_4_
  52.7 0.0 collective-permute-done.8.rest_2_
  52.7 0.0 collective-permute-done.9.rest_3_
  52.7 2.5 %out1.1 = bf16[512,1024]{1,0:T(8,128)(2,1)} custom-call(f32[1,1024]{1,0:T(1,128)} %bitcast.6, bf16[512,128]{1,0:T(8,128)(2,1)S(1)} %get-tuple-element.91.c_ref, f32[512,512]{1,0:T(8,128)S(1)} %get-tuple-element.92.plain_ref, f32[512,512]{1,0:T(8,128)S(1)} %get-tuple-element.93.slope_ref, ...), custom_call_target="tpu_custom_call", output_to_operand_aliasing={{}: (9, {})} | custom-call | flops 999999995904 | bytes 1 | tf_op jit(solution)/shard_map/out1/pallas_call | solution.py:485
  (8 shorter events, 0.0 us)
Async XLA Ops:
  1.6 4.4 %collective-permute-start = (bf16[4,6144]{1,0:T(4,128)(2,1)}, bf16[4,6144]{1,0:T(4,128)(2,1)}, u32[]{:S(2)}, u32[]{:S(2)}) collective-permute-start(bf16[4,6144]{1,0:T(4,128)(2,1)} %rim.1), channel_id=1, source_target_pairs={{0,1},{1,2},{2,3},{3,4},{4,5},{5,6},{6,7},{7,8},{8,9},{9,10},{10,1... | collective-permute-start | bytes 147464 | tf_op jit(solution)/shard_map/ppermute | solution.py:40
  8.8 11.3 %collective-permute-start.1 = (bf16[656,128]{1,0:T(8,128)(2,1)}, bf16[656,128]{1,0:T(8,128)(2,1)}, u32[]{:S(2)}, u32[]{:S(2)}) collective-permute-start(bf16[656,128]{1,0:T(8,128)(2,1)} %get-tuple-element.66), channel_id=1, source_target_pairs={{0,2},{1,3},{2,0},{3,1},{4,6},{5,7},{6,4},{7,5},{8,10},{9,11},{10,... | collective-permute-start | bytes 503816 | tf_op jit(solution)/shard_map/ppermute | solution.py:35
  13.0 7.2 %collective-permute-start.2 = (bf16[656,128]{1,0:T(8,128)(2,1)}, bf16[656,128]{1,0:T(8,128)(2,1)}, u32[]{:S(2)}, u32[]{:S(2)}) collective-permute-start(bf16[656,128]{1,0:T(8,128)(2,1)} %get-tuple-element.69), channel_id=1, source_target_pairs={{0,1},{1,0},{2,3},{3,2},{4,5},{5,4},{6,7},{7,6},{8,9},{9,8},{10,11... | collective-permute-start | bytes 503816 | tf_op jit(solution)/shard_map/ppermute | solution.py:35
  13.0 7.2 %collective-permute-start.3 = (bf16[656,128]{1,0:T(8,128)(2,1)}, bf16[656,128]{1,0:T(8,128)(2,1)}, u32[]{:S(2)}, u32[]{:S(2)}) collective-permute-start(bf16[656,128]{1,0:T(8,128)(2,1)} %get-tuple-element.71), channel_id=1, source_target_pairs={{0,3},{1,2},{2,1},{3,0},{4,7},{5,6},{6,5},{7,4},{8,11},{9,10},{10,... | collective-permute-start | bytes 503816 | tf_op jit(solution)/shard_map/ppermute | solution.py:35
  13.1 3.9 %copy-start = (bf16[128,4096]{1,0:T(8,128)(2,1)S(1)}, bf16[128,4096]{1,0:T(8,128)(2,1)}, u32[]{:S(2)}) copy-start(bf16[128,4096]{1,0:T(8,128)(2,1)} %z_ref) | copy-start | bytes 3145732
  18.0 14.4 %collective-permute-start.5 = (bf16[912,128]{1,0:T(8,128)(2,1)}, bf16[912,128]{1,0:T(8,128)(2,1)}, u32[]{:S(2)}, u32[]{:S(2)}) collective-permute-start(bf16[912,128]{1,0:T(8,128)(2,1)} %get-tuple-element.80), channel_id=1, source_target_pairs={{0,1},{1,0},{2,3},{3,2},{4,5},{5,4},{6,7},{7,6},{8,9},{9,8},{10,11... | collective-permute-start | bytes 700424 | tf_op jit(solution)/shard_map/ppermute | solution.py:35
  18.5 15.4 %collective-permute-start.6 = (bf16[912,128]{1,0:T(8,128)(2,1)}, bf16[912,128]{1,0:T(8,128)(2,1)}, u32[]{:S(2)}, u32[]{:S(2)}) collective-permute-start(bf16[912,128]{1,0:T(8,128)(2,1)} %get-tuple-element.81), channel_id=1, source_target_pairs={{0,2},{1,3},{2,0},{3,1},{4,6},{5,7},{6,4},{7,5},{8,10},{9,11},{10,... | collective-permute-start | bytes 700424 | tf_op jit(solution)/shard_map/ppermute | solution.py:35
  20.1 13.8 %collective-permute-start.7 = (bf16[912,128]{1,0:T(8,128)(2,1)}, bf16[912,128]{1,0:T(8,128)(2,1)}, u32[]{:S(2)}, u32[]{:S(2)}) collective-permute-start(bf16[912,128]{1,0:T(8,128)(2,1)} %get-tuple-element.82), channel_id=1, source_target_pairs={{0,3},{1,2},{2,1},{3,0},{4,7},{5,6},{6,5},{7,4},{8,11},{9,10},{10,... | collective-permute-start | bytes 700424 | tf_op jit(solution)/shard_map/ppermute | solution.py:35
  22.9 15.9 %collective-permute-start.4 = (bf16[528,128]{1,0:T(8,128)(2,1)}, bf16[528,128]{1,0:T(8,128)(2,1)}, u32[]{:S(2)}, u32[]{:S(2)}) collective-permute-start(bf16[528,128]{1,0:T(8,128)(2,1)} %get-tuple-element.72), channel_id=1, source_target_pairs={{0,4},{4,8},{8,12},{12,0},{1,5},{5,9},{9,13},{13,1},{2,6},{6,10},{... | collective-permute-start | bytes 405512 | tf_op jit(solution)/shard_map/ppermute | solution.py:352
  25.6 24.5 %collective-permute-start.11 = (bf16[528,128]{1,0:T(8,128)(2,1)}, bf16[528,128]{1,0:T(8,128)(2,1)}, u32[]{:S(2)}, u32[]{:S(2)}) collective-permute-start(bf16[528,128]{1,0:T(8,128)(2,1)} %get-tuple-element.72), channel_id=1, source_target_pairs={{0,8},{4,12},{8,0},{12,4},{1,9},{5,13},{9,1},{13,5},{2,10},{6,14},... | collective-permute-start | bytes 405512 | tf_op jit(solution)/shard_map/ppermute | solution.py:352
  28.2 18.7 %all-to-all-start = ((bf16[4,128,1024]{2,1,0:T(8,128)(2,1)}), bf16[4,128,1024]{2,1,0:T(8,128)(2,1)}, u32[]{:S(2)}, u32[]{:S(2)}) async-start(bf16[4,128,1024]{2,1,0:T(8,128)(2,1)} %gates.1), calls=%async_computation | async-start | bytes 2097152 | tf_op jit(solution)/shard_map/all_to_all | solution.py:456
  32.4 17.7 %collective-permute-start.12 = (bf16[528,128]{1,0:T(8,128)(2,1)}, bf16[528,128]{1,0:T(8,128)(2,1)}, u32[]{:S(2)}, u32[]{:S(2)}) collective-permute-start(bf16[528,128]{1,0:T(8,128)(2,1)} %get-tuple-element.72), channel_id=1, source_target_pairs={{0,12},{4,0},{8,4},{12,8},{1,13},{5,1},{9,5},{13,9},{2,14},{6,2},{... | collective-permute-start | bytes 405512 | tf_op jit(solution)/shard_map/ppermute | solution.py:352
  36.6 16.1 %collective-permute-start.10 = (bf16[528,128]{1,0:T(8,128)(2,1)}, bf16[528,128]{1,0:T(8,128)(2,1)}, u32[]{:S(2)}, u32[]{:S(2)}) collective-permute-start(bf16[528,128]{1,0:T(8,128)(2,1)} %get-tuple-element.96), channel_id=1, source_target_pairs={{0,12},{4,0},{8,4},{12,8},{1,13},{5,1},{9,5},{13,9},{2,14},{6,2},{... | collective-permute-start | bytes 405512 | tf_op jit(solution)/shard_map/ppermute | solution.py:352
  38.8 13.9 %collective-permute-start.8 = (bf16[528,128]{1,0:T(8,128)(2,1)}, bf16[528,128]{1,0:T(8,128)(2,1)}, u32[]{:S(2)}, u32[]{:S(2)}) collective-permute-start(bf16[528,128]{1,0:T(8,128)(2,1)} %get-tuple-element.96), channel_id=1, source_target_pairs={{0,4},{4,8},{8,12},{12,0},{1,5},{5,9},{9,13},{13,1},{2,6},{6,10},{... | collective-permute-start | bytes 405512 | tf_op jit(solution)/shard_map/ppermute | solution.py:352
  38.8 13.9 %collective-permute-start.9 = (bf16[528,128]{1,0:T(8,128)(2,1)}, bf16[528,128]{1,0:T(8,128)(2,1)}, u32[]{:S(2)}, u32[]{:S(2)}) collective-permute-start(bf16[528,128]{1,0:T(8,128)(2,1)} %get-tuple-element.96), channel_id=1, source_target_pairs={{0,8},{4,12},{8,0},{12,4},{1,9},{5,13},{9,1},{13,5},{2,10},{6,14},... | collective-permute-start | bytes 405512 | tf_op jit(solution)/shard_map/ppermute | solution.py:352

commit v4 on v3

--- a/solution.py
+++ b/solution.py
@@ -376,7 +376,7 @@
     shape = jax.ShapeDtypeStruct
 
     def trade(parts):
-        return [parts[0]] + [swap(parts[slot], slot) for slot in range(1, tp)]
+        return [parts[0]] + [swap(close(parts[slot]), slot) for slot in range(1, tp)]
 
     count = bc_input.shape[2]
     every = x_input.shape[1] + 2 * count

time: 55.7 us -> 55.7 us (level)
  no operation moved by 1% of the time
where the time goes in v4:
time: 55.7 us; the launch traced here: 55.3 us
  Pallas kernels  24.4 us (44%)
  starting transfers between devices  23.6 us (42%)
  waiting for transfers between devices  7.14 us (13%)
    pallas_call x6, Pallas kernels, call(): pl.pallas_call(kernel, in_specs=smem(scalars) + vmem(len(ins) - scalars),...  16.3 us
    ppermute x6, starting transfers between devices, scanned(): lax.ppermute(ship, 'ctx', [(i, (i + steps) % count) for i in range(count)])  9.89 us
    all_to_all x1, waiting for transfers between devices, shards(): gates = lax.all_to_all(gates, 'tp', split_axis=0, concat_axis=0, tiled=True)  7.11 us
    ppermute x6, starting transfers between devices, swap(): lax.ppermute(value, 'tp', [(i, i ^ slot) for i in range(lax.axis_size('tp...  6.51 us
    pallas_call x2, Pallas kernels, shards(): pl.pallas_call(functools.partial(out_kernel, spans, len(sent)), grid=(1,)...  5.08 us
    all_to_all x1, starting transfers between devices, shards(): gates = lax.all_to_all(gates, 'tp', split_axis=0, concat_axis=0, tiled=True)  4.24 us
    ppermute x1, starting transfers between devices, from_behind(): lax.ppermute(value, axis, [(i, i + steps) for i in range(count - steps)])  3 us
    pallas_call x1, Pallas kernels, shards(): pl.pallas_call(rim_kernel, grid=(1,), in_specs=[pl.BlockSpec((16, x_input...  1.56 us
  transfers between devices with their start and end apart: 14, of which 1 were waited for; matrix products, arithmetic and copies ran while one was open for 0% of the time, Pallas kernels for 32%

profile of v4, /device:TPU:0, one launch (start us, length us, event | category | flops | bytes accessed | tf_op | source)
XLA Modules:
  0.0 55.3 jit_solution(6493174614743102433)
XLA Ops:
  0.0 1.6 %rim.1 = bf16[4,6144]{1,0:T(4,128)(2,1)} custom-call(bf16[128,4096]{1,0:T(8,128)(2,1)} %refs_0_.1, bf16[128,2,1024]{2,1,0:T(2,128)(2,1)} %refs_1_.1), custom_call_target="tpu_custom_call" | custom-call | tf_op jit(solution)/shard_map/rim/pallas_call | solution.py:383
  1.6 3.0 %collective-permute-start = (bf16[4,6144]{1,0:T(4,128)(2,1)}, bf16[4,6144]{1,0:T(4,128)(2,1)}, u32[]{:S(2)}, u32[]{:S(2)}) collective-permute-start(bf16[4,6144]{1,0:T(4,128)(2,1)} %rim.1), channel_id=1, source_target_pairs={{0,1},{1,2},{2,3},{3,4},{4,5},{5,6},{6,7},{7,8},{8,9},{9,10},{10,1... | collective-permute-start | bytes 147464 | tf_op jit(solution)/shard_map/ppermute | solution.py:40
  4.6 1.4 %load.1 = (bf16[128,4096]{1,0:T(8,128)(2,1)S(1)}, bf16[128,2,1024]{2,1,0:T(2,128)(2,1)S(1)}, bf16[64,128]{1,0:T(8,128)(2,1)S(1)}, f32[4,4096]{1,0:T(4,128)S(1)},...) custom-call(bf16[128,4096]{1,0:T(8,128)(2,1)} %refs_0_.1, bf16[128,2,1024]{2,1,0:T(2,128)(2,1)} %refs_1_.1, ...), custom_call_target="tpu_custom_call" | custom-call | flops 999999995904 | bytes 1 | tf_op jit(solution)/shard_map/load/pallas_call | solution.py:402
  6.0 0.0 collective-permute-done.rim_ref
  6.0 2.8 %send0.1 = (bf16[656,128]{1,0:T(8,128)(2,1)S(1)}, bf16[656,128]{1,0:T(8,128)(2,1)}, bf16[656,128]{1,0:T(8,128)(2,1)}, bf16[656,128]{1,0:T(8,128)(2,1)}) custom-call(bf16[128,4096]{1,0:T(8,128)(2,1)S(1)} %get-tuple-element.54.x_ref, bf16[128,2,1024]{2,1,0:T(2,128)(2,1)S(1)} %get-tuple-element.55.bc_ref, bf16[64,128]{1,0:T(8,128)(2,1)S(1)} %get-tuple-element.56.dt_ref, ...), custom_call_target="tpu_custom_call" | custom-call | flops 999999995904 | bytes 1 | tf_op jit(solution)/shard_map/send0/pallas_call | solution.py:326
  8.8 4.2 %collective-permute-start.1 = (bf16[656,128]{1,0:T(8,128)(2,1)}, bf16[656,128]{1,0:T(8,128)(2,1)}, u32[]{:S(2)}, u32[]{:S(2)}) collective-permute-start(bf16[656,128]{1,0:T(8,128)(2,1)} %get-tuple-element.66), channel_id=1, source_target_pairs={{0,2},{1,3},{2,0},{3,1},{4,6},{5,7},{6,4},{7,5},{8,10},{9,11},{10,... | collective-permute-start | bytes 503816 | tf_op jit(solution)/shard_map/ppermute | solution.py:35
  13.0 0.1 collective-permute-start.3
  13.1 3.9 %send1.1 = (bf16[912,128]{1,0:T(8,128)(2,1)S(1)}, bf16[912,128]{1,0:T(8,128)(2,1)}, bf16[912,128]{1,0:T(8,128)(2,1)}, bf16[912,128]{1,0:T(8,128)(2,1)}) custom-call(bf16[128,4096]{1,0:T(8,128)(2,1)S(1)} %get-tuple-element.54.x_ref, bf16[128,2,1024]{2,1,0:T(2,128)(2,1)S(1)} %get-tuple-element.55.bc_ref, bf16[64,128]{1,0:T(8,128)(2,1)S(1)} %get-tuple-element.56.dt_ref, ...), custom_call_target="tpu_custom_call" | custom-call | flops 999999995904 | bytes 1 | tf_op jit(solution)/shard_map/send1/pallas_call | solution.py:326
  17.0 1.0 %gates.1 = bf16[4,128,1024]{2,1,0:T(8,128)(2,1)} custom-call(bf16[128,4096]{1,0:T(8,128)(2,1)S(1)} %copy-done), custom_call_target="tpu_custom_call" | custom-call | flops 1 | bytes 1 | tf_op jit(solution)/shard_map/gates/pallas_call | solution.py:326
  18.0 0.4 collective-permute-start.5
  18.5 1.6 %collective-permute-start.6 = (bf16[912,128]{1,0:T(8,128)(2,1)}, bf16[912,128]{1,0:T(8,128)(2,1)}, u32[]{:S(2)}, u32[]{:S(2)}) collective-permute-start(bf16[912,128]{1,0:T(8,128)(2,1)} %get-tuple-element.81), channel_id=1, source_target_pairs={{0,2},{1,3},{2,0},{3,1},{4,6},{5,7},{6,4},{7,5},{8,10},{9,11},{10,... | collective-permute-start | bytes 700424 | tf_op jit(solution)/shard_map/ppermute | solution.py:35
  20.1 0.1 collective-permute-start.7
  20.2 0.0 collective-permute-done.2.rest_1_
  20.2 0.0 collective-permute-done.3.rest_3_
  20.2 2.7 %state0.1 = (bf16[512,512]{1,0:T(8,128)(2,1)S(1)}, bf16[512,512]{1,0:T(8,128)(2,1)S(1)}, bf16[512,128]{1,0:T(8,128)(2,1)S(1)}, f32[4,8,128]{2,1,0:T(8,128)S(1)},...) custom-call(f32[16]{0:T(128)} %bias_ref.3, f32[16]{0:T(128)} %log_ref.3, ...), custom_call_target="tpu_custom_call" | custom-call | flops 999999995904 | bytes 1 | tf_op jit(solution)/shard_map/state0/pallas_call | solution.py:326
  22.9 2.7 %collective-permute-start.4 = (bf16[528,128]{1,0:T(8,128)(2,1)}, bf16[528,128]{1,0:T(8,128)(2,1)}, u32[]{:S(2)}, u32[]{:S(2)}) collective-permute-start(bf16[528,128]{1,0:T(8,128)(2,1)} %get-tuple-element.72), channel_id=1, source_target_pairs={{0,4},{4,8},{8,12},{12,0},{1,5},{5,9},{9,13},{13,1},{2,6},{6,10},{... | collective-permute-start | bytes 405512 | tf_op jit(solution)/shard_map/ppermute | solution.py:352
  25.6 2.6 %collective-permute-start.11 = (bf16[528,128]{1,0:T(8,128)(2,1)}, bf16[528,128]{1,0:T(8,128)(2,1)}, u32[]{:S(2)}, u32[]{:S(2)}) collective-permute-start(bf16[528,128]{1,0:T(8,128)(2,1)} %get-tuple-element.72), channel_id=1, source_target_pairs={{0,8},{4,12},{8,0},{12,4},{1,9},{5,13},{9,1},{13,5},{2,10},{6,14},... | collective-permute-start | bytes 405512 | tf_op jit(solution)/shard_map/ppermute | solution.py:352
  28.2 4.2 %all-to-all-start = ((bf16[4,128,1024]{2,1,0:T(8,128)(2,1)}), bf16[4,128,1024]{2,1,0:T(8,128)(2,1)}, u32[]{:S(2)}, u32[]{:S(2)}) async-start(bf16[4,128,1024]{2,1,0:T(8,128)(2,1)} %gates.1), calls=%async_computation | async-start | bytes 2097152 | tf_op jit(solution)/shard_map/all_to_all | solution.py:456
  32.4 0.0 collective-permute-done.5.rest_1_
  32.4 1.4 %collective-permute-start.12 = (bf16[528,128]{1,0:T(8,128)(2,1)}, bf16[528,128]{1,0:T(8,128)(2,1)}, u32[]{:S(2)}, u32[]{:S(2)}) collective-permute-start(bf16[528,128]{1,0:T(8,128)(2,1)} %get-tuple-element.72), channel_id=1, source_target_pairs={{0,12},{4,0},{8,4},{12,8},{1,13},{5,1},{9,5},{13,9},{2,14},{6,2},{... | collective-permute-start | bytes 405512 | tf_op jit(solution)/shard_map/ppermute | solution.py:352
  33.8 2.8 %state1.1 = (bf16[512,512]{1,0:T(8,128)(2,1)S(1)}, bf16[512,512]{1,0:T(8,128)(2,1)S(1)}, bf16[512,128]{1,0:T(8,128)(2,1)S(1)}, f32[4,8,128]{2,1,0:T(8,128)S(1)},...) custom-call(f32[16]{0:T(128)} %bias_ref.3, f32[16]{0:T(128)} %log_ref.3, ...), custom_call_target="tpu_custom_call" | custom-call | flops 999999995904 | bytes 1 | tf_op jit(solution)/shard_map/state1/pallas_call | solution.py:326
  36.6 2.2 %collective-permute-start.10 = (bf16[528,128]{1,0:T(8,128)(2,1)}, bf16[528,128]{1,0:T(8,128)(2,1)}, u32[]{:S(2)}, u32[]{:S(2)}) collective-permute-start(bf16[528,128]{1,0:T(8,128)(2,1)} %get-tuple-element.96), channel_id=1, source_target_pairs={{0,12},{4,0},{8,4},{12,8},{1,13},{5,1},{9,5},{13,9},{2,14},{6,2},{... | collective-permute-start | bytes 405512 | tf_op jit(solution)/shard_map/ppermute | solution.py:352
  38.8 0.0 collective-permute-start.8
  38.8 1.0 %collective-permute-start.9 = (bf16[528,128]{1,0:T(8,128)(2,1)}, bf16[528,128]{1,0:T(8,128)(2,1)}, u32[]{:S(2)}, u32[]{:S(2)}) collective-permute-start(bf16[528,128]{1,0:T(8,128)(2,1)} %get-tuple-element.96), channel_id=1, source_target_pairs={{0,8},{4,12},{8,0},{12,4},{1,9},{5,13},{9,1},{13,5},{2,10},{6,14},... | collective-permute-start | bytes 405512 | tf_op jit(solution)/shard_map/ppermute | solution.py:352
  39.8 7.1 %all-to-all-done.gate_ref = bf16[4,128,1024]{2,1,0:T(8,128)(2,1)} async-done(((bf16[4,128,1024]{2,1,0:T(8,128)(2,1)}), bf16[4,128,1024]{2,1,0:T(8,128)(2,1)}, u32[]{:S(2)}, u32[]{:S(2)}) %all-to-all-start) | async-done | bytes 1048608 | tf_op jit(solution)/shard_map/all_to_all | solution.py:456
  46.9 3.2 %mix.1 = (bf16[512,128]{1,0:T(8,128)(2,1)S(1)}, f32[512,512]{1,0:T(8,128)S(1)}, f32[512,512]{1,0:T(8,128)S(1)}, bf16[512,128]{1,0:T(8,128)(2,1)S(1)}, f32[512,512]{1,0:T(8,128)S(1)}, /*index=5*/f32[512,512]{1,0:T(8,128)S(1)}) custom-call(f32[16]{0:T(128)} %skip_ref.1, bf16[4,128,1024]{2,1,0:T(8,128)(2,1)} %all-to-all-done.gate_ref, ...), custom_call_target="tpu_custom_call" | custom-call | flops 999999995904 | bytes 1 | tf_op jit(solution)/shard_map/mix/pallas_call | solution.py:326
  50.1 0.0 collective-permute-done.11.rest_3_
  50.2 2.5 %out0.1.rest_5_ = bf16[512,1024]{1,0:T(8,128)(2,1)} custom-call(f32[1,1024]{1,0:T(1,128)} %bitcast.5, bf16[512,128]{1,0:T(8,128)(2,1)S(1)} %get-tuple-element.97.c_ref, f32[512,512]{1,0:T(8,128)S(1)} %get-tuple-element.98.plain_ref, f32[512,512]{1,0:T(8,128)S(1)} %get-tuple-element.99.slope_ref, f32[1,8,128]{2,1,0:T(8,128)S(1)} %get-tuple-element.100.rest_0_, ...), custom_call_target="tpu_custom_call" | custom-call | flops 999999995904 | bytes 1 | tf_op jit(solution)/shard_map/out0/pallas_call | solution.py:485
  52.7 0.0 collective-permute-done.10.rest_4_
  52.7 0.0 collective-permute-done.8.rest_2_
  52.7 0.0 collective-permute-done.9.rest_3_
  52.7 2.5 %out1.1 = bf16[512,1024]{1,0:T(8,128)(2,1)} custom-call(f32[1,1024]{1,0:T(1,128)} %bitcast.6, bf16[512,128]{1,0:T(8,128)(2,1)S(1)} %get-tuple-element.91.c_ref, f32[512,512]{1,0:T(8,128)S(1)} %get-tuple-element.92.plain_ref, f32[512,512]{1,0:T(8,128)S(1)} %get-tuple-element.93.slope_ref, ...), custom_call_target="tpu_custom_call", output_to_operand_aliasing={{}: (9, {})} | custom-call | flops 999999995904 | bytes 1 | tf_op jit(solution)/shard_map/out1/pallas_call | solution.py:485
  (8 shorter events, 0.0 us)
Async XLA Ops:
  1.6 4.4 %collective-permute-start = (bf16[4,6144]{1,0:T(4,128)(2,1)}, bf16[4,6144]{1,0:T(4,128)(2,1)}, u32[]{:S(2)}, u32[]{:S(2)}) collective-permute-start(bf16[4,6144]{1,0:T(4,128)(2,1)} %rim.1), channel_id=1, source_target_pairs={{0,1},{1,2},{2,3},{3,4},{4,5},{5,6},{6,7},{7,8},{8,9},{9,10},{10,1... | collective-permute-start | bytes 147464 | tf_op jit(solution)/shard_map/ppermute | solution.py:40
  8.8 11.3 %collective-permute-start.1 = (bf16[656,128]{1,0:T(8,128)(2,1)}, bf16[656,128]{1,0:T(8,128)(2,1)}, u32[]{:S(2)}, u32[]{:S(2)}) collective-permute-start(bf16[656,128]{1,0:T(8,128)(2,1)} %get-tuple-element.66), channel_id=1, source_target_pairs={{0,2},{1,3},{2,0},{3,1},{4,6},{5,7},{6,4},{7,5},{8,10},{9,11},{10,... | collective-permute-start | bytes 503816 | tf_op jit(solution)/shard_map/ppermute | solution.py:35
  13.0 7.2 %collective-permute-start.2 = (bf16[656,128]{1,0:T(8,128)(2,1)}, bf16[656,128]{1,0:T(8,128)(2,1)}, u32[]{:S(2)}, u32[]{:S(2)}) collective-permute-start(bf16[656,128]{1,0:T(8,128)(2,1)} %get-tuple-element.69), channel_id=1, source_target_pairs={{0,1},{1,0},{2,3},{3,2},{4,5},{5,4},{6,7},{7,6},{8,9},{9,8},{10,11... | collective-permute-start | bytes 503816 | tf_op jit(solution)/shard_map/ppermute | solution.py:35
  13.0 7.2 %collective-permute-start.3 = (bf16[656,128]{1,0:T(8,128)(2,1)}, bf16[656,128]{1,0:T(8,128)(2,1)}, u32[]{:S(2)}, u32[]{:S(2)}) collective-permute-start(bf16[656,128]{1,0:T(8,128)(2,1)} %get-tuple-element.71), channel_id=1, source_target_pairs={{0,3},{1,2},{2,1},{3,0},{4,7},{5,6},{6,5},{7,4},{8,11},{9,10},{10,... | collective-permute-start | bytes 503816 | tf_op jit(solution)/shard_map/ppermute | solution.py:35
  13.1 3.9 %copy-start = (bf16[128,4096]{1,0:T(8,128)(2,1)S(1)}, bf16[128,4096]{1,0:T(8,128)(2,1)}, u32[]{:S(2)}) copy-start(bf16[128,4096]{1,0:T(8,128)(2,1)} %z_ref) | copy-start | bytes 3145732
  18.0 14.4 %collective-permute-start.5 = (bf16[912,128]{1,0:T(8,128)(2,1)}, bf16[912,128]{1,0:T(8,128)(2,1)}, u32[]{:S(2)}, u32[]{:S(2)}) collective-permute-start(bf16[912,128]{1,0:T(8,128)(2,1)} %get-tuple-element.80), channel_id=1, source_target_pairs={{0,1},{1,0},{2,3},{3,2},{4,5},{5,4},{6,7},{7,6},{8,9},{9,8},{10,11... | collective-permute-start | bytes 700424 | tf_op jit(solution)/shard_map/ppermute | solution.py:35
  18.5 15.4 %collective-permute-start.6 = (bf16[912,128]{1,0:T(8,128)(2,1)}, bf16[912,128]{1,0:T(8,128)(2,1)}, u32[]{:S(2)}, u32[]{:S(2)}) collective-permute-start(bf16[912,128]{1,0:T(8,128)(2,1)} %get-tuple-element.81), channel_id=1, source_target_pairs={{0,2},{1,3},{2,0},{3,1},{4,6},{5,7},{6,4},{7,5},{8,10},{9,11},{10,... | collective-permute-start | bytes 700424 | tf_op jit(solution)/shard_map/ppermute | solution.py:35
  20.1 13.8 %collective-permute-start.7 = (bf16[912,128]{1,0:T(8,128)(2,1)}, bf16[912,128]{1,0:T(8,128)(2,1)}, u32[]{:S(2)}, u32[]{:S(2)}) collective-permute-start(bf16[912,128]{1,0:T(8,128)(2,1)} %get-tuple-element.82), channel_id=1, source_target_pairs={{0,3},{1,2},{2,1},{3,0},{4,7},{5,6},{6,5},{7,4},{8,11},{9,10},{10,... | collective-permute-start | bytes 700424 | tf_op jit(solution)/shard_map/ppermute | solution.py:35
  22.9 15.9 %collective-permute-start.4 = (bf16[528,128]{1,0:T(8,128)(2,1)}, bf16[528,128]{1,0:T(8,128)(2,1)}, u32[]{:S(2)}, u32[]{:S(2)}) collective-permute-start(bf16[528,128]{1,0:T(8,128)(2,1)} %get-tuple-element.72), channel_id=1, source_target_pairs={{0,4},{4,8},{8,12},{12,0},{1,5},{5,9},{9,13},{13,1},{2,6},{6,10},{... | collective-permute-start | bytes 405512 | tf_op jit(solution)/shard_map/ppermute | solution.py:352
  25.6 24.5 %collective-permute-start.11 = (bf16[528,128]{1,0:T(8,128)(2,1)}, bf16[528,128]{1,0:T(8,128)(2,1)}, u32[]{:S(2)}, u32[]{:S(2)}) collective-permute-start(bf16[528,128]{1,0:T(8,128)(2,1)} %get-tuple-element.72), channel_id=1, source_target_pairs={{0,8},{4,12},{8,0},{12,4},{1,9},{5,13},{9,1},{13,5},{2,10},{6,14},... | collective-permute-start | bytes 405512 | tf_op jit(solution)/shard_map/ppermute | solution.py:352
  28.2 18.7 %all-to-all-start = ((bf16[4,128,1024]{2,1,0:T(8,128)(2,1)}), bf16[4,128,1024]{2,1,0:T(8,128)(2,1)}, u32[]{:S(2)}, u32[]{:S(2)}) async-start(bf16[4,128,1024]{2,1,0:T(8,128)(2,1)} %gates.1), calls=%async_computation | async-start | bytes 2097152 | tf_op jit(solution)/shard_map/all_to_all | solution.py:456
  32.4 17.7 %collective-permute-start.12 = (bf16[528,128]{1,0:T(8,128)(2,1)}, bf16[528,128]{1,0:T(8,128)(2,1)}, u32[]{:S(2)}, u32[]{:S(2)}) collective-permute-start(bf16[528,128]{1,0:T(8,128)(2,1)} %get-tuple-element.72), channel_id=1, source_target_pairs={{0,12},{4,0},{8,4},{12,8},{1,13},{5,1},{9,5},{13,9},{2,14},{6,2},{... | collective-permute-start | bytes 405512 | tf_op jit(solution)/shard_map/ppermute | solution.py:352
  36.6 16.1 %collective-permute-start.10 = (bf16[528,128]{1,0:T(8,128)(2,1)}, bf16[528,128]{1,0:T(8,128)(2,1)}, u32[]{:S(2)}, u32[]{:S(2)}) collective-permute-start(bf16[528,128]{1,0:T(8,128)(2,1)} %get-tuple-element.96), channel_id=1, source_target_pairs={{0,12},{4,0},{8,4},{12,8},{1,13},{5,1},{9,5},{13,9},{2,14},{6,2},{... | collective-permute-start | bytes 405512 | tf_op jit(solution)/shard_map/ppermute | solution.py:352
  38.8 13.9 %collective-permute-start.8 = (bf16[528,128]{1,0:T(8,128)(2,1)}, bf16[528,128]{1,0:T(8,128)(2,1)}, u32[]{:S(2)}, u32[]{:S(2)}) collective-permute-start(bf16[528,128]{1,0:T(8,128)(2,1)} %get-tuple-element.96), channel_id=1, source_target_pairs={{0,4},{4,8},{8,12},{12,0},{1,5},{5,9},{9,13},{13,1},{2,6},{6,10},{... | collective-permute-start | bytes 405512 | tf_op jit(solution)/shard_map/ppermute | solution.py:352
  38.8 13.9 %collective-permute-start.9 = (bf16[528,128]{1,0:T(8,128)(2,1)}, bf16[528,128]{1,0:T(8,128)(2,1)}, u32[]{:S(2)}, u32[]{:S(2)}) collective-permute-start(bf16[528,128]{1,0:T(8,128)(2,1)} %get-tuple-element.96), channel_id=1, source_target_pairs={{0,8},{4,12},{8,0},{12,4},{1,9},{5,13},{9,1},{13,5},{2,10},{6,14},... | collective-permute-start | bytes 405512 | tf_op jit(solution)/shard_map/ppermute | solution.py:352
